TPU v7x, 128 devices: a whole 4x4x4 slice. The times are simulated.
128 devices in a mesh: dp: 32 (over x_lo, z, y), tensor: 4 (over x_hi, core).
Axes of the slice: x: 4 (x_hi: 2, x_lo: 2; x = x_hi * 2 + x_lo), y: 4, z: 4, core: 2. Of those that a mesh axis runs over, the one named last changes fastest.
Arguments:
- inputs: bfloat16 [8192, 1024], P('dp'), may hold values from -6 to 6
- segments: int32 [32, 256], P('dp'), may hold values from 0 to 3, as said below
- positions: int32 [32, 256], P('dp'), may hold values from 0 to 127, as said below
- w_query: bfloat16 [2, 1024, 2048], P(None, None, 'tensor'), may hold values from -0.1875 to 0.1875
- key_weight: bfloat16 [2, 1024, 1024], P(None, None, 'tensor'), may hold values from -0.1875 to 0.1875
- value_weight: bfloat16 [2, 1024, 1024], P(None, None, 'tensor'), may hold values from -0.1875 to 0.1875
- w_out: bfloat16 [2, 2048, 1024], P(None, 'tensor'), may hold values from -0.75 to 0.75
- w_gate: bfloat16 [2, 1024, 3072], P(None, None, 'tensor'), may hold values from -0.1875 to 0.1875
- w_up: bfloat16 [2, 1024, 3072], P(None, None, 'tensor'), may hold values from -0.1875 to 0.1875
- w_down: bfloat16 [2, 3072, 1024], P(None, 'tensor'), may hold values from -0.109375 to 0.109375
- gain_in: float32 [2, 1024], replicated, may hold values from 0.25 to 1.75
- gain_post: float32 [2, 1024], replicated, may hold values from 0.25 to 1.75
- gain_query: float32 [2, 128], replicated, may hold values from 0.5 to 2
- gain_key: float32 [2, 128], replicated, may hold values from 0.5 to 2
- cotangent: bfloat16 [8192, 1024], P('dp'), may hold values from -1.5 to 1.5
Outputs:
- block_out: float32 [8192, 1024], P('dp')
- input_grad: float32 [8192, 1024], P('dp')
- grad_w_query: float32 [2, 1024, 2048], P(None, 'dp', 'tensor')
- grad_w_key: float32 [2, 1024, 1024], P(None, 'dp', 'tensor')
- grad_w_value: float32 [2, 1024, 1024], P(None, 'dp', 'tensor')
- grad_w_out: float32 [2, 2048, 1024], P(None, 'tensor', 'dp')
- grad_w_gate: float32 [2, 1024, 3072], P(None, 'dp', 'tensor')
- grad_w_up: float32 [2, 1024, 3072], P(None, 'dp', 'tensor')
- grad_w_down: float32 [2, 3072, 1024], P(None, 'tensor', 'dp')
- grad_gain_in: float32 [2, 1024], P(None, 'dp')
- grad_gain_post: float32 [2, 1024], P(None, 'dp')
- grad_gain_query: float32 [2, 128], P(None, 'dp')
- grad_gain_key: float32 [2, 128], P(None, 'dp')
Inputs may be any that keep to these rules, and one draw needn't show every extreme that they name: `segments`: along each packed row the segment numbers start at 0, never fall, and take exactly four values; every segment holds at most 128 tokens, and in every row one segment holds exactly that many. `positions`: each token's index within its segment, 0 at a segment's first token.
All inputs are finite; a program needn't handle non-finite values.
Results may differ from a plain program's by a relative error of at most 0.025.
Values sent between devices are 32-bit elements; how exact they have to be, the bound alone decides.
No kernel may reach another device: no remote copies, remote signals or barrier semaphores. Data moves between devices by JAX's collectives and lax.ppermute only.
A program may use at most 192 MiB of HBM per device.

v0:
```python
import jax
import jax.numpy as jnp
from jax import lax
from jax.sharding import PartitionSpec as P

EPS = 1e-06
THETA = 1000000.0
NEG_FILL = -1e30


def inv_rms(values):
    return lax.rsqrt(jnp.mean(values * values, axis=-1, keepdims=True) + EPS)


def norm_back(upstream, normed, scale_inv, gain):
    scaled = upstream * gain
    return scale_inv * (scaled - normed * jnp.mean(scaled * normed, axis=-1, keepdims=True))


def rope_tables(position_ids, head_dim):
    half_dim = head_dim // 2
    inverse_freq = THETA ** (-(jnp.arange(half_dim).astype(jnp.float32) * 2.0 / head_dim))
    angles = position_ids.astype(jnp.float32)[:, None] * inverse_freq[None, :]
    return (jnp.cos(angles)[:, None, :], jnp.sin(angles)[:, None, :])


def rotate(values, cosine, sine):
    half_dim = values.shape[-1] // 2
    lower_half = values[..., :half_dim]
    upper_half = values[..., half_dim:]
    return jnp.concatenate(
        [lower_half * cosine - upper_half * sine, upper_half * cosine + lower_half * sine], axis=-1
    )


def rotate_back(values, cosine, sine):
    half_dim = values.shape[-1] // 2
    lower_half = values[..., :half_dim]
    upper_half = values[..., half_dim:]
    return jnp.concatenate(
        [lower_half * cosine + upper_half * sine, upper_half * cosine - lower_half * sine], axis=-1
    )


def contract(form, left, right):
    return jnp.einsum(form, left, right, preferred_element_type=jnp.float32)


def row_scores(q_part, k_rot, segment_row, first_row, score_scale):
    rows_here = q_part.shape[0]
    scores = contract("qkgd,skd->kgqs", q_part, k_rot) * score_scale
    query_ids = first_row + jnp.arange(rows_here)
    key_ids = jnp.arange(k_rot.shape[0])
    allowed = (segment_row[first_row : first_row + rows_here, None] == segment_row[None, :]) & (
        key_ids[None, :] <= query_ids[:, None]
    )
    return jnp.where(allowed, scores, NEG_FILL)


def attention_forward(q_rot, k_rot, values, segment_row):
    length, kv_heads, head_dim = k_rot.shape
    groups = q_rot.shape[1] // kv_heads
    block_rows = min(512, length)
    score_scale = head_dim ** (-0.5)
    q_part = q_rot.reshape(block_rows, kv_heads, groups, head_dim)
    scores = row_scores(q_part, k_rot, segment_row, 0, score_scale)
    row_peak = jnp.max(scores, axis=-1, keepdims=True)
    log_total = row_peak + jnp.log(jnp.sum(jnp.exp(scores - row_peak), axis=-1, keepdims=True))
    weights = jnp.exp(scores - log_total).astype(jnp.bfloat16)
    attended = contract("kgqs,skd->qkgd", weights, values)
    outputs = attended.reshape(block_rows, -1).astype(jnp.bfloat16)
    return (outputs, log_total)


def attention_backward(q_rot, k_rot, values, attended, grad_attended, log_totals, segment_row):
    length, kv_heads, head_dim = k_rot.shape
    groups = q_rot.shape[1] // kv_heads
    block_rows = min(512, length)
    score_scale = head_dim ** (-0.5)
    q_part = q_rot.reshape(block_rows, kv_heads, groups, head_dim)
    go_part = grad_attended.reshape(block_rows, kv_heads, groups, head_dim)
    o_part = attended.reshape(block_rows, kv_heads, groups, head_dim)
    scores = row_scores(q_part, k_rot, segment_row, 0, score_scale)
    probs = jnp.exp(scores - log_totals)
    weights = probs.astype(jnp.bfloat16)
    grad_values = contract("kgqs,qkgd->skd", weights, go_part)
    grad_probs = contract("qkgd,skd->kgqs", go_part, values)
    row_dots = contract("qkgd,qkgd->kgq", go_part, o_part)
    grad_scores = (probs * (grad_probs - row_dots[..., None]) * score_scale).astype(jnp.bfloat16)
    grad_queries = contract("kgqs,skd->qkgd", grad_scores, k_rot).reshape(
        block_rows, kv_heads * groups, head_dim
    )
    grad_keys = contract("kgqs,qkgd->skd", grad_scores, q_part)
    return (grad_queries, grad_keys, grad_values)


def layer_forward(resid, segment_row, cosine, sine, params):
    (
        w_query,
        key_weight,
        value_weight,
        w_out,
        w_gate,
        w_up,
        w_down,
        gain_in,
        gain_post,
        gain_query,
        gain_key,
    ) = params
    length = resid.shape[0]
    head_dim = gain_query.shape[0]
    scale_in = inv_rms(resid)
    normed_in = resid * scale_in
    attn_input = (normed_in * gain_in).astype(jnp.bfloat16)
    queries = jnp.dot(attn_input, w_query, preferred_element_type=jnp.float32).reshape(
        length, -1, head_dim
    )
    keys_raw = jnp.dot(attn_input, key_weight, preferred_element_type=jnp.float32).reshape(
        length, -1, head_dim
    )
    values = (
        jnp.dot(attn_input, value_weight, preferred_element_type=jnp.float32)
        .astype(jnp.bfloat16)
        .reshape(length, -1, head_dim)
    )
    q_scale = inv_rms(queries)
    q_normed = queries * q_scale
    k_scale = inv_rms(keys_raw)
    k_normed = keys_raw * k_scale
    q_rot = rotate(q_normed * gain_query, cosine, sine).astype(jnp.bfloat16)
    k_rot = rotate(k_normed * gain_key, cosine, sine).astype(jnp.bfloat16)
    attended, log_totals = attention_forward(q_rot, k_rot, values, segment_row)
    attn_share = lax.psum_scatter(
        jnp.dot(attended, w_out, preferred_element_type=jnp.float32),
        "tensor",
        scatter_dimension=0,
        tiled=True,
    )
    attn_sum = lax.all_gather(attn_share, "tensor", axis=0, tiled=True)
    middle = resid + attn_sum
    scale_post = inv_rms(middle)
    normed_post = middle * scale_post
    mlp_input = (normed_post * gain_post).astype(jnp.bfloat16)
    gate_logits = jnp.dot(mlp_input, w_gate, preferred_element_type=jnp.float32)
    up_pre = jnp.dot(mlp_input, w_up, preferred_element_type=jnp.float32)
    hidden = (jax.nn.silu(gate_logits) * up_pre).astype(jnp.bfloat16)
    mlp_share = lax.psum_scatter(
        jnp.dot(hidden, w_down, preferred_element_type=jnp.float32),
        "tensor",
        scatter_dimension=0,
        tiled=True,
    )
    mlp_sum = lax.all_gather(mlp_share, "tensor", axis=0, tiled=True)
    result = middle + mlp_sum
    saved = (
        scale_in,
        normed_in,
        attn_input,
        q_scale,
        q_normed,
        k_scale,
        k_normed,
        q_rot,
        k_rot,
        values,
        attended,
        log_totals,
        scale_post,
        normed_post,
        mlp_input,
        gate_logits,
        up_pre,
        hidden,
    )
    return (result, saved)


def layer_backward(upstream, saved, params, segment_row, cosine, sine):
    (
        w_query,
        key_weight,
        value_weight,
        w_out,
        w_gate,
        w_up,
        w_down,
        gain_in,
        gain_post,
        gain_query,
        gain_key,
    ) = params
    (
        scale_in,
        normed_in,
        attn_input,
        q_scale,
        q_normed,
        k_scale,
        k_normed,
        q_rot,
        k_rot,
        values,
        attended,
        log_totals,
        scale_post,
        normed_post,
        mlp_input,
        gate_logits,
        up_pre,
        hidden,
    ) = saved
    length = upstream.shape[0]
    upstream_bf = upstream.astype(jnp.bfloat16)
    grad_down = jnp.dot(hidden.T, upstream_bf, preferred_element_type=jnp.float32)
    grad_hidden = jnp.dot(upstream_bf, w_down.T, preferred_element_type=jnp.float32)
    sigma = jax.nn.sigmoid(gate_logits)
    grad_gate_pre = (grad_hidden * up_pre * sigma * (1.0 + gate_logits * (1.0 - sigma))).astype(
        jnp.bfloat16
    )
    grad_up_pre = (grad_hidden * gate_logits * sigma).astype(jnp.bfloat16)
    grad_gate = jnp.dot(mlp_input.T, grad_gate_pre, preferred_element_type=jnp.float32)
    grad_upward = jnp.dot(mlp_input.T, grad_up_pre, preferred_element_type=jnp.float32)
    mlp_partial = jnp.dot(grad_gate_pre, w_gate.T, preferred_element_type=jnp.float32) + jnp.dot(
        grad_up_pre, w_up.T, preferred_element_type=jnp.float32
    )
    mlp_back_share = lax.psum_scatter(mlp_partial, "tensor", scatter_dimension=0, tiled=True)
    grad_mlp_in = lax.all_gather(mlp_back_share, "tensor", axis=0, tiled=True)
    grad_gain_post = jnp.sum(grad_mlp_in * normed_post, axis=0)
    grad_middle = upstream + norm_back(grad_mlp_in, normed_post, scale_post, gain_post)
    middle_bf = grad_middle.astype(jnp.bfloat16)
    grad_output = jnp.dot(attended.T, middle_bf, preferred_element_type=jnp.float32)
    grad_attended = jnp.dot(middle_bf, w_out.T, preferred_element_type=jnp.float32).astype(
        jnp.bfloat16
    )
    grad_q_rot, grad_k_rot, grad_v_raw = attention_backward(
        q_rot, k_rot, values, attended, grad_attended, log_totals, segment_row
    )
    grad_q_normed = rotate_back(grad_q_rot, cosine, sine)
    grad_k_normed = rotate_back(grad_k_rot, cosine, sine)
    query_gain_part = jnp.sum(grad_q_normed * q_normed, axis=(0, 1))
    key_gain_part = jnp.sum(grad_k_normed * k_normed, axis=(0, 1))
    grad_queries = (
        norm_back(grad_q_normed, q_normed, q_scale, gain_query)
        .astype(jnp.bfloat16)
        .reshape(length, -1)
    )
    grad_keys = (
        norm_back(grad_k_normed, k_normed, k_scale, gain_key)
        .astype(jnp.bfloat16)
        .reshape(length, -1)
    )
    grad_values = grad_v_raw.astype(jnp.bfloat16).reshape(length, -1)
    query_gradient = jnp.dot(attn_input.T, grad_queries, preferred_element_type=jnp.float32)
    grad_key = jnp.dot(attn_input.T, grad_keys, preferred_element_type=jnp.float32)
    grad_value = jnp.dot(attn_input.T, grad_values, preferred_element_type=jnp.float32)
    attn_partial = (
        jnp.dot(grad_queries, w_query.T, preferred_element_type=jnp.float32)
        + jnp.dot(grad_keys, key_weight.T, preferred_element_type=jnp.float32)
        + jnp.dot(grad_values, value_weight.T, preferred_element_type=jnp.float32)
    )
    shares = (
        lax.psum_scatter(attn_partial, "tensor", scatter_dimension=0, tiled=True),
        lax.psum_scatter(query_gain_part, "tensor", scatter_dimension=0, tiled=True),
        lax.psum_scatter(key_gain_part, "tensor", scatter_dimension=0, tiled=True),
    )
    grad_attn_in, grad_gain_query, grad_gain_key = (
        lax.all_gather(shares[0], "tensor", axis=0, tiled=True),
        lax.all_gather(shares[1], "tensor", axis=0, tiled=True),
        lax.all_gather(shares[2], "tensor", axis=0, tiled=True),
    )
    grad_gain_in = jnp.sum(grad_attn_in * normed_in, axis=0)
    grad_resid = grad_middle + norm_back(grad_attn_in, normed_in, scale_in, gain_in)
    return (
        grad_resid,
        (
            query_gradient,
            grad_key,
            grad_value,
            grad_output,
            grad_gate,
            grad_upward,
            grad_down,
            grad_gain_in,
            grad_gain_post,
            grad_gain_query,
            grad_gain_key,
        ),
    )


def shards(
    inputs,
    segments,
    positions,
    w_query,
    key_weight,
    value_weight,
    w_out,
    w_gate,
    w_up,
    w_down,
    gain_in,
    gain_post,
    gain_query,
    gain_key,
    cotangent,
):
    all_params = (
        w_query,
        key_weight,
        value_weight,
        w_out,
        w_gate,
        w_up,
        w_down,
        gain_in,
        gain_post,
        gain_query,
        gain_key,
    )
    layer_count = w_query.shape[0]
    segment_row = segments[0]
    cosine, sine = rope_tables(positions[0], gain_query.shape[1])
    resid = inputs.astype(jnp.float32)
    saves = []
    for layer_idx in range(layer_count):
        params = tuple((member[layer_idx] for member in all_params))
        resid, saved = layer_forward(resid, segment_row, cosine, sine, params)
        saves.append(saved)
    upstream = cotangent.astype(jnp.float32)
    collected = []
    for layer_idx in reversed(range(layer_count)):
        params = tuple((member[layer_idx] for member in all_params))
        upstream, terms = layer_backward(
            upstream, saves[layer_idx], params, segment_row, cosine, sine
        )
        collected.insert(0, terms)
    stacked = tuple(
        (
            jnp.stack([layer_terms[member_idx] for layer_terms in collected])
            for member_idx in range(11)
        )
    )
    stacked = (
        lax.psum_scatter(stacked[0], "dp", scatter_dimension=1, tiled=True),
        lax.psum_scatter(stacked[1], "dp", scatter_dimension=1, tiled=True),
        lax.psum_scatter(stacked[2], "dp", scatter_dimension=1, tiled=True),
        lax.psum_scatter(stacked[3], "dp", scatter_dimension=2, tiled=True),
        lax.psum_scatter(stacked[4], "dp", scatter_dimension=1, tiled=True),
        lax.psum_scatter(stacked[5], "dp", scatter_dimension=1, tiled=True),
        lax.psum_scatter(stacked[6], "dp", scatter_dimension=2, tiled=True),
        lax.psum_scatter(stacked[7], "dp", scatter_dimension=1, tiled=True),
        lax.psum_scatter(stacked[8], "dp", scatter_dimension=1, tiled=True),
        lax.psum_scatter(stacked[9], "dp", scatter_dimension=1, tiled=True),
        lax.psum_scatter(stacked[10], "dp", scatter_dimension=1, tiled=True),
    )
    return (
        resid,
        upstream,
        stacked[0],
        stacked[1],
        stacked[2],
        stacked[3],
        stacked[4],
        stacked[5],
        stacked[6],
        stacked[7],
        stacked[8],
        stacked[9],
        stacked[10],
    )


def solution(mesh):
    return jax.shard_map(
        shards,
        mesh=mesh,
        in_specs=(
            P("dp", None),
            P("dp", None),
            P("dp", None),
            P(None, None, "tensor"),
            P(None, None, "tensor"),
            P(None, None, "tensor"),
            P(None, "tensor", None),
            P(None, None, "tensor"),
            P(None, None, "tensor"),
            P(None, "tensor", None),
            P(),
            P(),
            P(),
            P(),
            P("dp", None),
        ),
        out_specs=(
            P("dp", None),
            P("dp", None),
            P(None, "dp", "tensor"),
            P(None, "dp", "tensor"),
            P(None, "dp", "tensor"),
            P(None, "tensor", "dp"),
            P(None, "dp", "tensor"),
            P(None, "dp", "tensor"),
            P(None, "tensor", "dp"),
            P(None, "dp"),
            P(None, "dp"),
            P(None, "dp"),
            P(None, "dp"),
        ),
        check_vma=False,
    )
```

profile of v0, /device:TPU:0, one launch (start us, length us, event | category | flops | bytes accessed | tf_op | source)
XLA Modules:
  0.0 2063.6 jit_solution(15970232604039339013)
XLA Ops:
  9.3 2.7 slice_bitcast_fusion
  12.6 1.6 convolution_convert_fusion.5
  20.8 34.3 %reduce-scatter.22.cloned.1.call-done = f32[64,1024]{1,0:T(8,128)} async-done(((f32[256,1024]{1,0:T(8,128)}), f32[64,1024]{1,0:T(8,128)}) %reduce-scatter.22.cloned.1.call-update) | async-done | bytes 262160 | tf_op jit(solution)/shard_map/reduce_scatter | solution.py:134
  55.8 21.2 %all-gather.9.cloned.1.call-done = f32[256,1024]{1,0:T(8,128)} async-done(((f32[64,1024]{1,0:T(8,128)}), f32[256,1024]{1,0:T(8,128)}) %all-gather.9.cloned.1.call-update) | async-done | bytes 1048592 | tf_op jit(solution)/shard_map/all_gather | solution.py:140
  76.9 1.6 multiply_reduce_fusion.8
  78.7 2.2 fusion.22
  83.4 1.5 fusion.14
  85.0 31.3 %reduce-scatter.24.cloned.1.call-done = f32[64,1024]{1,0:T(8,128)} async-done(((f32[256,1024]{1,0:T(8,128)}), f32[64,1024]{1,0:T(8,128)}) %reduce-scatter.24.cloned.1.call-update) | async-done | bytes 262160 | tf_op jit(solution)/shard_map/reduce_scatter | solution.py:148
  117.7 2.0 copy.62
  119.7 18.3 all-gather.11.cloned.1.call-done
  138.0 1.6 multiply_reduce_fusion.7
  144.0 1.7 multiply_reduce_fusion.21
  152.2 31.2 %reduce-scatter.26.cloned.1.call-done = f32[64,1024]{1,0:T(8,128)} async-done(((f32[256,1024]{1,0:T(8,128)}), f32[64,1024]{1,0:T(8,128)}) %reduce-scatter.26.cloned.1.call-update) | async-done | bytes 262160 | tf_op jit(solution)/shard_map/reduce_scatter | solution.py:134
  183.6 3.1 fusion
  186.7 18.4 all-gather.13.cloned.1.call-done
  205.1 1.6 multiply_reduce_fusion.6
  209.5 1.6 multiply_convert_fusion.6
  212.0 1.6 fusion.43
  213.6 3.1 fusion.2
  216.8 28.1 %reduce-scatter.30.cloned.1.call-done = f32[64,1024]{1,0:T(8,128)} async-done(((f32[256,1024]{1,0:T(8,128)}), f32[64,1024]{1,0:T(8,128)}) %reduce-scatter.30.cloned.1.call-update) | async-done | bytes 262160 | tf_op jit(solution)/shard_map/reduce_scatter | solution.py:227
  244.9 33.7 %reduce-scatter.28.cloned.1.call-done = f32[64,1024]{1,0:T(8,128)} async-done(((f32[256,1024]{1,0:T(8,128)}), f32[64,1024]{1,0:T(8,128)}) %reduce-scatter.28.cloned.1.call-update) | async-done | bytes 262160 | tf_op jit(solution)/shard_map/reduce_scatter | solution.py:148
  278.7 21.8 %all-gather.17.cloned.1.call-done = f32[256,1024]{1,0:T(8,128)} async-done(((f32[64,1024]{1,0:T(8,128)}), f32[256,1024]{1,0:T(8,128)}) %all-gather.17.cloned.1.call-update) | async-done | bytes 1048592 | tf_op jit(solution)/shard_map/all_gather | solution.py:228
  300.5 2.5 multiply_reduce_fusion
  303.6 18.6 all-gather.15.cloned.1.call-done
  322.3 3.5 multiply_add_fusion.2
  327.9 1.7 reshape.273
  329.6 1.8 copy.73
  331.5 1.9 bitcast_convert_fusion.1
  333.4 2.0 copy.98
  336.8 1.8 fusion.57
  344.9 31.2 %reduce-scatter.32.cloned.1.call-done = f32[64,1024]{1,0:T(8,128)} async-done(((f32[256,1024]{1,0:T(8,128)}), f32[64,1024]{1,0:T(8,128)}) %reduce-scatter.32.cloned.1.call-update) | async-done | bytes 262160 | tf_op jit(solution)/shard_map/reduce_scatter | solution.py:263
  376.2 21.7 %all-gather.19.cloned.1.call-done = f32[256,1024]{1,0:T(8,128)} async-done(((f32[64,1024]{1,0:T(8,128)}), f32[256,1024]{1,0:T(8,128)}) %all-gather.19.cloned.1.call-update) | async-done | bytes 1048592 | tf_op jit(solution)/shard_map/all_gather | solution.py:268
  397.9 2.3 multiply_reduce_fusion.2
  400.3 1.8 multiply_add_fusion.1
  403.0 1.6 copy-done.39
  405.6 1.6 fusion.40
  407.3 31.2 %reduce-scatter.34.cloned.1.call-done = f32[64,1024]{1,0:T(8,128)} async-done(((f32[256,1024]{1,0:T(8,128)}), f32[64,1024]{1,0:T(8,128)}) %reduce-scatter.34.cloned.1.call-update) | async-done | bytes 262160 | tf_op jit(solution)/shard_map/reduce_scatter | solution.py:227
  438.8 21.4 %all-gather.21.cloned.1.call-done = f32[256,1024]{1,0:T(8,128)} async-done(((f32[64,1024]{1,0:T(8,128)}), f32[256,1024]{1,0:T(8,128)}) %all-gather.21.cloned.1.call-update) | async-done | bytes 1048592 | tf_op jit(solution)/shard_map/all_gather | solution.py:228
  460.2 2.3 multiply_reduce_fusion.1
  462.6 1.8 multiply_add_fusion
  470.9 1.7 convolution_bitcast_fusion.17
  476.7 31.3 %reduce-scatter.36.cloned.1.call-done = f32[64,1024]{1,0:T(8,128)} async-done(((f32[256,1024]{1,0:T(8,128)}), f32[64,1024]{1,0:T(8,128)}) %reduce-scatter.36.cloned.1.call-update) | async-done | bytes 262160 | tf_op jit(solution)/shard_map/reduce_scatter | solution.py:263
  508.1 1.9 convolution_bitcast_fusion
  510.0 1.8 convolution_bitcast_fusion.6
  512.3 3.3 pad_maximum_fusion.2
  515.7 10.4 copy.83
  527.1 1.9 convolution_bitcast_fusion.7
  529.7 1.7 fusion.65
  532.5 4.9 pad_maximum_fusion.4
  537.3 7.2 copy.82
  551.8 2.4 pad_maximum_fusion.3
  556.7 3.0 pad_maximum_fusion
  561.9 3.1 pad_maximum_fusion.1
  569.5 7.4 all-reduce.15
  577.5 7.2 all-reduce.14
  584.7 83.1 %all-reduce.12 = (f32[2,128]{1,0:T(2,128)S(1)}, f32[2,128]{1,0:T(2,128)S(1)}) all-reduce(f32[2,128]{1,0:T(2,128)S(1)} %pad_maximum_fusion.19, f32[2,128]{1,0:T(2,128)S(1)} %pad_maximum_fusion.20), channel_id=21, replica_groups=mesh['dp'=32,'tensor'=4] {'dp'}, use_global_device_ids=true, to_apply=%region_45.46.clone | all-reduce | flops 512 | bytes 4096
  668.4 25.7 %reduce-scatter.50.cloned.1.call-done = f32[32,2]{1,0:T(8,128)} async-done(((f32[1024,2]{1,0:T(8,128)}), f32[32,2]{1,0:T(8,128)}) %reduce-scatter.50.cloned.1.call-update) | async-done | bytes 272
  696.7 157.7 %reduce-scatter.48.cloned.1.call-done = f32[32,2]{1,0:T(8,128)} async-done(((f32[1024,2]{1,0:T(8,128)}), f32[32,2]{1,0:T(8,128)}) %reduce-scatter.48.cloned.1.call-update) | async-done | bytes 272
  855.8 350.0 %all-reduce.18.cloned.1.call-done = (f32[2,512,1024]{1,0,2:T(2,128)}, f32[2,768,1024]{1,0,2:T(2,128)}) async-done(((f32[2,512,1024]{1,0,2:T(2,128)}, f32[2,768,1024]{1,0,2:T(2,128)}), (f32[2,512,1024]{1,0,2:T(2,128)}, f32[2,768,1024]{1,0,2:T(2,128)})) %all-reduce.18.cloned.1.call-update) | async-done | bytes 10485776
  1209.0 163.5 %reduce-scatter.40.cloned.1.call-done = f32[2,32,256]{2,1,0:T(8,128)} async-done(((f32[2,1024,256]{2,1,0:T(8,128)}), f32[2,32,256]{2,1,0:T(8,128)}) %reduce-scatter.40.cloned.1.call-update) | async-done | bytes 65552 | tf_op jit(solution)/shard_map/reduce_scatter | solution.py:347
  1372.6 164.4 %reduce-scatter.42.cloned.1.call-done = f32[2,32,256]{2,1,0:T(8,128)} async-done(((f32[2,1024,256]{2,1,0:T(8,128)}), f32[2,32,256]{2,1,0:T(8,128)}) %reduce-scatter.42.cloned.1.call-update) | async-done | bytes 65552 | tf_op jit(solution)/shard_map/reduce_scatter | solution.py:348
  1537.0 169.2 %reduce-scatter.38.cloned.1.call-done = f32[2,32,512]{2,1,0:T(8,128)} async-done(((f32[2,1024,512]{2,1,0:T(8,128)}), f32[2,32,512]{2,1,0:T(8,128)}) %reduce-scatter.38.cloned.1.call-update) | async-done | bytes 131088 | tf_op jit(solution)/shard_map/reduce_scatter | solution.py:346
  1706.2 175.1 %reduce-scatter.44.cloned.1.call-done = f32[2,32,768]{2,1,0:T(8,128)} async-done(((f32[2,1024,768]{2,1,0:T(8,128)}), f32[2,32,768]{2,1,0:T(8,128)}) %reduce-scatter.44.cloned.1.call-update) | async-done | bytes 196624 | tf_op jit(solution)/shard_map/reduce_scatter | solution.py:350
  1881.3 175.0 %reduce-scatter.46.cloned.1.call-done = f32[2,32,768]{2,1,0:T(8,128)} async-done(((f32[2,1024,768]{2,1,0:T(8,128)}), f32[2,32,768]{2,1,0:T(8,128)}) %reduce-scatter.46.cloned.1.call-update) | async-done | bytes 196624 | tf_op jit(solution)/shard_map/reduce_scatter | solution.py:351
  (424 shorter events, 76.5 us)
Async XLA Ops:
  7.2 47.9 %reduce-scatter.22.cloned.1.call-start = ((), (), s32[]{:S(2)}) async-start(), calls=%async_computation.15 | async-start | bytes 1310720 | tf_op jit(solution)/shard_map/reduce_scatter | solution.py:134
  8.0 131.6 %copy-start.82 = (f32[1,1024]{1,0:T(1,128)}, f32[1,1024]{1,0:T(1,128)S(1)}, u32[]{:S(2)}) copy-start(f32[1,1024]{1,0:T(1,128)S(1)} %get-tuple-element.102) | copy-start | bytes 12292
  9.3 7.5 copy-start.87
  14.1 4.7 copy-start.78
  14.8 126.6 %copy-start.103 = (f32[128]{0:T(128)}, f32[128]{0:T(128)S(1)}, u32[]{:S(2)}) copy-start(f32[128]{0:T(128)S(1)} %get-tuple-element.106) | copy-start | bytes 1540
  18.6 36.5 %copy-start.105 = (f32[2,1024]{1,0:T(2,128)S(1)}, f32[2,1024]{1,0:T(2,128)}, u32[]{:S(2)}) copy-start(f32[2,1024]{1,0:T(2,128)} %param.26) | copy-start | bytes 24580
  19.2 59.3 %copy-start.31 = (bf16[2,128,2,256]{3,1,2,0:T(8,128)(2,1)}, bf16[2,128,2,256]{3,1,2,0:T(8,128)(2,1)S(1)}, u32[]{:S(2)}) copy-start(bf16[2,128,2,256]{3,1,2,0:T(8,128)(2,1)S(1)} %convolution_convert_fusion.3) | copy-start | bytes 786436
  20.7 56.2 %all-gather.9.cloned.1.call-start = ((), (), s32[]{:S(2)}) async-start(), calls=%async_computation.16 | async-start | bytes 1310720 | tf_op jit(solution)/shard_map/all_gather | solution.py:140
  55.1 61.2 %reduce-scatter.24.cloned.1.call-start = ((), (), s32[]{:S(2)}) async-start(), calls=%async_computation.17 | async-start | bytes 1310720 | tf_op jit(solution)/shard_map/reduce_scatter | solution.py:148
  55.8 25.1 %copy-start.84 = (f32[1,1024]{1,0:T(1,128)}, f32[1,1024]{1,0:T(1,128)S(1)}, u32[]{:S(2)}) copy-start(f32[1,1024]{1,0:T(1,128)S(1)} %get-tuple-element.101) | copy-start | bytes 12292
  76.9 4.0 copy-start.37
  83.4 32.9 %copy-start.30 = (bf16[512,1024]{0,1:T(8,128)(2,1)S(1)}, bf16[512,1024]{0,1:T(8,128)(2,1)}, u32[]{:S(2)}) copy-start(bf16[512,1024]{0,1:T(8,128)(2,1)} %get-tuple-element.73) | copy-start | bytes 3145732
  85.0 53.0 %all-gather.11.cloned.1.call-start = ((), (), s32[]{:S(2)}) async-start(), calls=%async_computation.18 | async-start | bytes 1310720 | tf_op jit(solution)/shard_map/all_gather | solution.py:154
  116.3 67.1 %reduce-scatter.26.cloned.1.call-start = ((), (), s32[]{:S(2)}) async-start(), calls=%async_computation.19 | async-start | bytes 1310720 | tf_op jit(solution)/shard_map/reduce_scatter | solution.py:134
  141.3 7.3 copy-start.80
  144.0 5.6 copy-start.79
  144.0 6.7 copy-start.12
  152.1 53.0 %all-gather.13.cloned.1.call-start = ((), (), s32[]{:S(2)}) async-start(), calls=%async_computation.20 | async-start | bytes 1310720 | tf_op jit(solution)/shard_map/all_gather | solution.py:140
  183.4 61.4 %reduce-scatter.30.cloned.1.call-start = ((), (), s32[]{:S(2)}) async-start(), calls=%async_computation.23 | async-start | bytes 1310720 | tf_op jit(solution)/shard_map/reduce_scatter | solution.py:227
  206.7 4.4 copy-start.8
  213.6 65.1 %reduce-scatter.28.cloned.1.call-start = ((), (), s32[]{:S(2)}) async-start(), calls=%async_computation.21 | async-start | bytes 1310720 | tf_op jit(solution)/shard_map/reduce_scatter | solution.py:148
  216.7 83.8 %all-gather.17.cloned.1.call-start = ((), (), s32[]{:S(2)}) async-start(), calls=%async_computation.24 | async-start | bytes 1310720 | tf_op jit(solution)/shard_map/all_gather | solution.py:228
  244.9 77.4 %all-gather.15.cloned.1.call-start = ((), (), s32[]{:S(2)}) async-start(), calls=%async_computation.22 | async-start | bytes 1310720 | tf_op jit(solution)/shard_map/all_gather | solution.py:154
  278.7 97.5 %reduce-scatter.32.cloned.1.call-start = ((), (), s32[]{:S(2)}) async-start(), calls=%async_computation.25 | async-start | bytes 1310720 | tf_op jit(solution)/shard_map/reduce_scatter | solution.py:263
  322.3 4.5 copy-start.13
  335.4 4.3 copy-start.44
  335.4 4.3 copy-start.45
  335.4 4.8 copy-start.1
  335.4 4.8 copy-start.48
  336.7 3.9 copy-start.18
  336.8 3.9 copy-start.81
  336.8 3.9 copy-start.104
  342.9 55.0 %copy-start.83 = (f32[1,1024]{1,0:T(1,128)S(1)}, f32[1,1024]{1,0:T(1,128)}, u32[]{:S(2)}) copy-start(f32[1,1024]{1,0:T(1,128)} %copy-done.82) | copy-start | bytes 12292
  342.9 55.0 %copy-start.96 = (f32[256]{0:T(256)S(1)}, f32[256]{0:T(256)}, u32[]{:S(2)}) copy-start(f32[256]{0:T(256)} %copy-done.95) | copy-start | bytes 3076
  344.9 53.0 %all-gather.19.cloned.1.call-start = ((), (), s32[]{:S(2)}) async-start(), calls=%async_computation.26 | async-start | bytes 1310720 | tf_op jit(solution)/shard_map/all_gather | solution.py:268
  376.2 62.3 %reduce-scatter.34.cloned.1.call-start = ((), (), s32[]{:S(2)}) async-start(), calls=%async_computation.27 | async-start | bytes 1310720 | tf_op jit(solution)/shard_map/reduce_scatter | solution.py:227
  397.9 4.2 copy-start.36
  397.9 4.2 copy-start.119
  397.9 4.2 copy-start.121
  405.3 55.0 %copy-start.85 = (f32[1,1024]{1,0:T(1,128)S(1)}, f32[1,1024]{1,0:T(1,128)}, u32[]{:S(2)}) copy-start(f32[1,1024]{1,0:T(1,128)} %copy-done.84) | copy-start | bytes 12292
  405.3 54.9 %copy-start.94 = (f32[256]{0:T(256)S(1)}, f32[256]{0:T(256)}, u32[]{:S(2)}) copy-start(f32[256]{0:T(256)} %copy-done.93) | copy-start | bytes 3076
  407.2 53.0 %all-gather.21.cloned.1.call-start = ((), (), s32[]{:S(2)}) async-start(), calls=%async_computation.28 | async-start | bytes 1310720 | tf_op jit(solution)/shard_map/all_gather | solution.py:228
  438.5 69.4 %reduce-scatter.36.cloned.1.call-start = ((), (), s32[]{:S(2)}) async-start(), calls=%async_computation.29 | async-start | bytes 1310720 | tf_op jit(solution)/shard_map/reduce_scatter | solution.py:263
  460.2 4.2 copy-start.14
  467.1 5.4 copy-start.49
  468.3 4.7 copy-start.20
  468.3 4.7 copy-start.102
  476.6 33.3 %copy-start.7 = (f32[256,1024]{1,0:T(8,128)S(1)}, f32[256,1024]{1,0:T(8,128)}, u32[]{:S(2)}) copy-start(f32[256,1024]{1,0:T(8,128)} %copy-done.6) | copy-start | bytes 3145732
  476.7 53.0 %all-gather.23.cloned.1.call-start = ((), (), s32[]{:S(2)}) async-start(), calls=%async_computation.30 | async-start | bytes 1310720 | tf_op jit(solution)/shard_map/all_gather | solution.py:268
  508.0 186.1 %reduce-scatter.50.cloned.1.call-start = ((), (), s32[]{:S(2)}) async-start(), calls=%async_computation.37 | async-start | bytes 540672
  515.7 10.4 copy-start.98
  515.7 10.4 copy-start.100
  526.1 5.3 copy-start.99
  529.0 325.4 %reduce-scatter.48.cloned.1.call-start = ((), (), s32[]{:S(2)}) async-start(), calls=%async_computation.36 | async-start | bytes 540672
  532.4 673.4 %all-reduce.18.cloned.1.call-start = ((), (), s32[]{:S(2)}) async-start(), calls=%async_computation.38 | async-start | bytes 20971520
  544.6 828.0 %reduce-scatter.40.cloned.1.call-start = ((), (), s32[]{:S(2)}) async-start(), calls=%async_computation.32 | async-start | bytes 2162688 | tf_op jit(solution)/shard_map/reduce_scatter | solution.py:347
  547.9 989.1 %reduce-scatter.42.cloned.1.call-start = ((), (), s32[]{:S(2)}) async-start(), calls=%async_computation.33 | async-start | bytes 2162688 | tf_op jit(solution)/shard_map/reduce_scatter | solution.py:348
  550.3 1155.9 %reduce-scatter.38.cloned.1.call-start = ((), (), s32[]{:S(2)}) async-start(), calls=%async_computation.31 | async-start | bytes 4325376 | tf_op jit(solution)/shard_map/reduce_scatter | solution.py:346
  554.3 1327.1 %reduce-scatter.44.cloned.1.call-start = ((), (), s32[]{:S(2)}) async-start(), calls=%async_computation.34 | async-start | bytes 6488064 | tf_op jit(solution)/shard_map/reduce_scatter | solution.py:350
  559.7 1496.6 %reduce-scatter.46.cloned.1.call-start = ((), (), s32[]{:S(2)}) async-start(), calls=%async_computation.35 | async-start | bytes 6488064 | tf_op jit(solution)/shard_map/reduce_scatter | solution.py:351
  565.0 4.4 copy-start.110
  565.0 4.5 copy-start.111
  565.0 4.5 copy-start.113
  565.0 130.4 %copy-start.29 = (f32[256,1024]{1,0:T(8,128)S(1)}, f32[256,1024]{1,0:T(8,128)}, u32[]{:S(2)}) copy-start(f32[256,1024]{1,0:T(8,128)} %all-gather.23.cloned.1.call-done) | copy-start | bytes 3145732
  (82 other events, 158.5 us)
Sparse Core Ops, SparseCore 0:
  20.8 34.1 reduce-scatter.21
  56.7 20.1 all-gather.8
  85.1 31.1 reduce-scatter.23
  117.8 20.1 all-gather.10
  152.2 31.1 reduce-scatter.25
  184.9 20.1 all-gather.12
  213.7 31.1 reduce-scatter.29
  247.5 31.1 reduce-scatter.27
  280.3 20.1 all-gather.16
  302.1 20.1 all-gather.14
  345.0 31.1 reduce-scatter.31
  377.7 20.1 all-gather.18
  407.3 31.1 reduce-scatter.33
  440.0 20.1 all-gather.20
  476.8 31.1 reduce-scatter.35
  509.5 20.1 all-gather.22
  532.4 161.6 reduce-scatter.49
  696.3 158.0 reduce-scatter.47
  857.0 348.7 all-reduce.17
  1208.6 163.9 reduce-scatter.39
  1375.5 161.4 reduce-scatter.41
  1540.0 166.2 reduce-scatter.37
  1709.2 172.0 reduce-scatter.43
  1884.2 172.0 reduce-scatter.45
where the time goes:
time: 2070 us; the launch traced here: 2060 us
  waiting for transfers between devices  1780 us (86%)
  blocking collectives  97.6 us (5%)
  local copies, waits for them, and re-layouts  61 us (3%)
  matrix products  55.5 us (3%)
  other arithmetic  53.3 us (3%)
    unnamed x27, waiting for transfers between devices  534 us
    reduce_scatter x1, waiting for transfers between devices, shards(): lax.psum_scatter(stacked[4], 'dp', scatter_dimension=1, tiled=True)  175 us
    reduce_scatter x1, waiting for transfers between devices, shards(): lax.psum_scatter(stacked[5], 'dp', scatter_dimension=1, tiled=True)  175 us
    reduce_scatter x1, waiting for transfers between devices, shards(): lax.psum_scatter(stacked[0], 'dp', scatter_dimension=1, tiled=True)  169 us
    reduce_scatter x1, waiting for transfers between devices, shards(): lax.psum_scatter(stacked[2], 'dp', scatter_dimension=1, tiled=True)  164 us
    reduce_scatter x1, waiting for transfers between devices, shards(): lax.psum_scatter(stacked[1], 'dp', scatter_dimension=1, tiled=True)  164 us
    unnamed x3, blocking collectives  97.6 us
    reduce_scatter x2, waiting for transfers between devices, layer_forward(): lax.psum_scatter(jnp.dot(attended, w_out, preferred_element_type=jnp.floa...  65.5 us
  transfers between devices with their start and end apart: 24, of which 24 were waited for; matrix products, arithmetic and copies ran while one was open for 4% of the time, Pallas kernels for 0%

commit v1 on v0

v1 whole, which is shorter than its diff:
```python
import jax
import jax.numpy as jnp
from jax import lax
from jax.experimental import pallas as pl
from jax.experimental.pallas import tpu as pltpu
from jax.sharding import Mesh, PartitionSpec as P

EPS = 1e-06
THETA = 1000000.0
NEG_FILL = -1e30


def inv_rms(values):
    return lax.rsqrt(jnp.mean(values * values, axis=-1, keepdims=True) + EPS)


def norm_back(upstream, normed, scale_inv, gain):
    scaled = upstream * gain
    return scale_inv * (scaled - normed * jnp.mean(scaled * normed, axis=-1, keepdims=True))


def rope_tables(position_ids, head_dim):
    half_dim = head_dim // 2
    inverse_freq = THETA ** (-(jnp.arange(half_dim).astype(jnp.float32) * 2.0 / head_dim))
    angles = position_ids.astype(jnp.float32)[:, None] * inverse_freq[None, :]
    return (jnp.cos(angles)[:, None, :], jnp.sin(angles)[:, None, :])


def rotate(values, cosine, sine):
    half_dim = values.shape[-1] // 2
    lower_half = values[..., :half_dim]
    upper_half = values[..., half_dim:]
    return jnp.concatenate(
        [lower_half * cosine - upper_half * sine, upper_half * cosine + lower_half * sine], axis=-1
    )


def rotate_back(values, cosine, sine):
    half_dim = values.shape[-1] // 2
    lower_half = values[..., :half_dim]
    upper_half = values[..., half_dim:]
    return jnp.concatenate(
        [lower_half * cosine + upper_half * sine, upper_half * cosine - lower_half * sine], axis=-1
    )


def contract(form, left, right):
    return jnp.einsum(form, left, right, preferred_element_type=jnp.float32)


SWAP = ((0, 1), (1, 0))


def row_scores(q_part, k_rot, allowed, score_scale):
    scores = contract("qkgd,skd->kgqs", q_part, k_rot) * score_scale
    return jnp.where(allowed, scores, NEG_FILL)


def attention_forward(q_rot, k_rot, values, allowed):
    length, kv_heads, head_dim = k_rot.shape
    groups = q_rot.shape[1] // kv_heads
    score_scale = head_dim ** (-0.5)
    q_part = q_rot.reshape(length, kv_heads, groups, head_dim)
    scores = row_scores(q_part, k_rot, allowed, score_scale)
    row_peak = jnp.max(scores, axis=-1, keepdims=True)
    log_total = row_peak + jnp.log(jnp.sum(jnp.exp(scores - row_peak), axis=-1, keepdims=True))
    probs = jnp.exp(scores - log_total)
    attended = contract("kgqs,skd->qkgd", probs.astype(jnp.bfloat16), values)
    outputs = attended.reshape(length, -1).astype(jnp.bfloat16)
    return (outputs, log_total)


def attention_backward(q_rot, k_rot, values, attended, grad_attended, log_totals, allowed):
    length, kv_heads, head_dim = k_rot.shape
    groups = q_rot.shape[1] // kv_heads
    score_scale = head_dim ** (-0.5)
    q_part = q_rot.reshape(length, kv_heads, groups, head_dim)
    go_part = grad_attended.reshape(length, kv_heads, groups, head_dim)
    o_part = attended.reshape(length, kv_heads, groups, head_dim)
    scores = row_scores(q_part, k_rot, allowed, score_scale)
    probs = jnp.exp(scores - log_totals)
    weights = probs.astype(jnp.bfloat16)
    grad_values = contract("kgqs,qkgd->skd", weights, go_part)
    grad_probs = contract("qkgd,skd->kgqs", go_part, values)
    row_dots = contract("qkgd,qkgd->kgq", go_part, o_part)
    grad_scores = (probs * (grad_probs - row_dots[..., None]) * score_scale).astype(jnp.bfloat16)
    grad_queries = contract("kgqs,skd->qkgd", grad_scores, k_rot).reshape(
        length, kv_heads * groups, head_dim
    )
    grad_keys = contract("kgqs,qkgd->skd", grad_scores, q_part)
    return (grad_queries, grad_keys, grad_values)


def group_sum(partial):
    half = partial.shape[0] // 2
    own = partial[:half] + lax.ppermute(partial[half:], "core", SWAP)
    own = own + lax.ppermute(own, "x_hi", SWAP)
    return jnp.concatenate([own, lax.ppermute(own, "core", SWAP)], axis=0)


def weight_grads(pairs):
    tokens, width = pairs[0][0].shape
    lefts = []
    for left, _ in pairs:
        if not any(left is seen for seen in lefts):
            lefts.append(left)
    which = [next(i for i, seen in enumerate(lefts) if seen is left) for left, _ in pairs]
    rights = [right for _, right in pairs]
    columns = [right.shape[1] for right in rights]
    total = sum(columns)
    n_left = len(lefts)
    tile = 256
    halves = width // 2
    per_half = halves // tile

    def body(*refs):
        left_refs = refs[:n_left]
        right_refs = refs[n_left:-1]
        out_ref = refs[-1]
        start = 0
        for idx, right_ref in enumerate(right_refs):
            piece = lax.dot_general(
                left_refs[which[idx]][...],
                right_ref[...],
                (((0,), (0,)), ((), ())),
                preferred_element_type=jnp.float32,
            )
            out_ref[:, 0, :, start : start + columns[idx]] = piece.reshape(
                tile // 32, 32, columns[idx]
            )
            start += columns[idx]

    flops = 2 * tokens * width * total
    out = pl.pallas_call(
        body,
        grid=(2 * per_half,),
        in_specs=[pl.BlockSpec((tokens, tile), lambda i: (0, i)) for _ in lefts]
        + [pl.BlockSpec((tokens, c), lambda i: (0, 0)) for c in columns],
        out_specs=pl.BlockSpec(
            (tile // 32, 1, 32, total), lambda i: (i % per_half, i // per_half, 0, 0)
        ),
        out_shape=jax.ShapeDtypeStruct((width // 64, 2, 32, total), jnp.float32),
        cost_estimate=pl.CostEstimate(
            flops=flops, transcendentals=0, bytes_accessed=4 * width * total
        ),
        name="weight_grads",
    )(*lefts, *rights)
    return out.reshape(width, total)


def scatter_rows(stacked):
    part = lax.psum_scatter(stacked, ("z", "y"), scatter_dimension=0, tiled=True)
    rows = part.shape[0] // 2
    part = part.reshape(2, rows, part.shape[1])
    mine = lax.axis_index("x_lo")
    keep = lax.dynamic_index_in_dim(part, mine, 0, keepdims=False)
    send = lax.dynamic_index_in_dim(part, 1 - mine, 0, keepdims=False)
    return keep + lax.ppermute(send, "x_lo", SWAP)


def sum_everywhere(small):
    for axis in ("x_lo", "y", "z"):
        size = lax.axis_size(axis)
        step = 1
        while step < size:
            small = small + lax.ppermute(small, axis, [(i, i ^ step) for i in range(size)])
            step *= 2
    for axis in ("core", "x_hi"):
        small = small + lax.ppermute(small, axis, SWAP)
    return small


def layer_forward(resid, allowed, cosine, sine, params):
    (w_query, key_weight, value_weight, w_out, w_gate, w_up, w_down) = params[:7]
    (gain_in, gain_post, gain_query, gain_key) = params[7:]
    length = resid.shape[0]
    head_dim = gain_query.shape[0]
    scale_in = inv_rms(resid)
    normed_in = resid * scale_in
    attn_input = (normed_in * gain_in).astype(jnp.bfloat16)
    queries = jnp.dot(attn_input, w_query, preferred_element_type=jnp.float32).reshape(
        length, -1, head_dim
    )
    keys_raw = jnp.dot(attn_input, key_weight, preferred_element_type=jnp.float32).reshape(
        length, -1, head_dim
    )
    values = (
        jnp.dot(attn_input, value_weight, preferred_element_type=jnp.float32)
        .astype(jnp.bfloat16)
        .reshape(length, -1, head_dim)
    )
    q_scale = inv_rms(queries)
    q_normed = queries * q_scale
    k_scale = inv_rms(keys_raw)
    k_normed = keys_raw * k_scale
    q_rot = rotate(q_normed * gain_query, cosine, sine).astype(jnp.bfloat16)
    k_rot = rotate(k_normed * gain_key, cosine, sine).astype(jnp.bfloat16)
    attended, log_totals = attention_forward(q_rot, k_rot, values, allowed)
    attn_sum = group_sum(jnp.dot(attended, w_out, preferred_element_type=jnp.float32))
    middle = resid + attn_sum
    scale_post = inv_rms(middle)
    normed_post = middle * scale_post
    mlp_input = (normed_post * gain_post).astype(jnp.bfloat16)
    gate_logits = jnp.dot(mlp_input, w_gate, preferred_element_type=jnp.float32)
    up_pre = jnp.dot(mlp_input, w_up, preferred_element_type=jnp.float32)
    hidden = (jax.nn.silu(gate_logits) * up_pre).astype(jnp.bfloat16)
    mlp_sum = group_sum(jnp.dot(hidden, w_down, preferred_element_type=jnp.float32))
    result = middle + mlp_sum
    saved = (
        scale_in,
        normed_in,
        attn_input,
        q_scale,
        q_normed,
        k_scale,
        k_normed,
        q_rot,
        k_rot,
        values,
        attended,
        log_totals,
        scale_post,
        normed_post,
        mlp_input,
        gate_logits,
        up_pre,
        hidden,
    )
    return (result, saved)


def layer_backward(upstream, saved, params, allowed, cosine, sine):
    (w_query, key_weight, value_weight, w_out, w_gate, w_up, w_down) = params[:7]
    (gain_in, gain_post, gain_query, gain_key) = params[7:]
    (
        scale_in,
        normed_in,
        attn_input,
        q_scale,
        q_normed,
        k_scale,
        k_normed,
        q_rot,
        k_rot,
        values,
        attended,
        log_totals,
        scale_post,
        normed_post,
        mlp_input,
        gate_logits,
        up_pre,
        hidden,
    ) = saved
    length = upstream.shape[0]
    upstream_bf = upstream.astype(jnp.bfloat16)
    grad_hidden = jnp.dot(upstream_bf, w_down.T, preferred_element_type=jnp.float32)
    sigma = jax.nn.sigmoid(gate_logits)
    grad_gate_pre = (grad_hidden * up_pre * sigma * (1.0 + gate_logits * (1.0 - sigma))).astype(
        jnp.bfloat16
    )
    grad_up_pre = (grad_hidden * gate_logits * sigma).astype(jnp.bfloat16)
    mlp_partial = jnp.dot(grad_gate_pre, w_gate.T, preferred_element_type=jnp.float32) + jnp.dot(
        grad_up_pre, w_up.T, preferred_element_type=jnp.float32
    )
    grad_mlp_in = group_sum(mlp_partial)
    mlp_grads = scatter_rows(
        weight_grads(
            [(mlp_input, grad_gate_pre), (mlp_input, grad_up_pre), (upstream_bf, hidden)]
        )
    )
    grad_gain_post = jnp.sum(mlp_partial * normed_post, axis=0)
    grad_middle = upstream + norm_back(grad_mlp_in, normed_post, scale_post, gain_post)
    middle_bf = grad_middle.astype(jnp.bfloat16)
    grad_attended = jnp.dot(middle_bf, w_out.T, preferred_element_type=jnp.float32).astype(
        jnp.bfloat16
    )
    grad_q_rot, grad_k_rot, grad_v_raw = attention_backward(
        q_rot, k_rot, values, attended, grad_attended, log_totals, allowed
    )
    grad_q_normed = rotate_back(grad_q_rot, cosine, sine)
    grad_k_normed = rotate_back(grad_k_rot, cosine, sine)
    query_gain_part = jnp.sum(grad_q_normed * q_normed, axis=(0, 1))
    key_gain_part = jnp.sum(grad_k_normed * k_normed, axis=(0, 1))
    grad_queries = (
        norm_back(grad_q_normed, q_normed, q_scale, gain_query)
        .astype(jnp.bfloat16)
        .reshape(length, -1)
    )
    grad_keys = (
        norm_back(grad_k_normed, k_normed, k_scale, gain_key)
        .astype(jnp.bfloat16)
        .reshape(length, -1)
    )
    grad_values = grad_v_raw.astype(jnp.bfloat16).reshape(length, -1)
    attn_partial = (
        jnp.dot(grad_queries, w_query.T, preferred_element_type=jnp.float32)
        + jnp.dot(grad_keys, key_weight.T, preferred_element_type=jnp.float32)
        + jnp.dot(grad_values, value_weight.T, preferred_element_type=jnp.float32)
    )
    attn_grads = scatter_rows(
        weight_grads(
            [
                (attn_input, grad_queries),
                (attn_input, grad_keys),
                (attn_input, grad_values),
                (middle_bf, attended),
            ]
        )
    )
    grad_attn_in = group_sum(attn_partial)
    grad_gain_in = jnp.sum(attn_partial * normed_in, axis=0)
    grad_resid = grad_middle + norm_back(grad_attn_in, normed_in, scale_in, gain_in)
    gains = (grad_gain_in, grad_gain_post, query_gain_part, key_gain_part)
    return (grad_resid, mlp_grads, attn_grads, gains)


def split_columns(stacked, sizes):
    pieces = []
    start = 0
    for size in sizes:
        pieces.append(stacked[:, start : start + size])
        start += size
    return pieces


def shards(
    inputs,
    segments,
    positions,
    w_query,
    key_weight,
    value_weight,
    w_out,
    w_gate,
    w_up,
    w_down,
    gain_in,
    gain_post,
    gain_query,
    gain_key,
    cotangent,
):
    all_params = (
        w_query,
        key_weight,
        value_weight,
        w_out,
        w_gate,
        w_up,
        w_down,
        gain_in,
        gain_post,
        gain_query,
        gain_key,
    )
    layer_count = w_query.shape[0]
    length = segments.shape[1]
    width = inputs.shape[1]
    half = length // 2
    core = lax.axis_index("core")

    def turn(values):
        return jnp.where(core == 0, values, jnp.concatenate([values[half:], values[:half]], axis=0))

    segment_row = turn(segments[0])
    index_row = turn(jnp.arange(length))
    allowed = (segment_row[:, None] == segment_row[None, :]) & (
        index_row[None, :] <= index_row[:, None]
    )
    cosine, sine = rope_tables(turn(positions[0]), gain_query.shape[1])
    resid = turn(inputs).astype(jnp.float32)
    saves = []
    for layer_idx in range(layer_count):
        params = tuple((member[layer_idx] for member in all_params))
        resid, saved = layer_forward(resid, allowed, cosine, sine, params)
        saves.append(saved)
    upstream = turn(cotangent).astype(jnp.float32)
    mlp_rows, attn_rows, gains = ([], [], [])
    for layer_idx in reversed(range(layer_count)):
        params = tuple((member[layer_idx] for member in all_params))
        upstream, mlp_part, attn_part, gain_part = layer_backward(
            upstream, saves[layer_idx], params, allowed, cosine, sine
        )
        mlp_rows.insert(0, mlp_part)
        attn_rows.insert(0, attn_part)
        gains.insert(0, gain_part)
    sizes = [member.shape[1] for group in gains for member in [g[None] for g in group]]
    flat = sum_everywhere(
        jnp.concatenate([member for group in gains for member in group]).reshape(-1, 128)
    ).reshape(-1)
    place = lax.axis_index(("x_lo", "z", "y"))
    n_place = lax.axis_size(("x_lo", "z", "y"))
    gain_pieces = []
    start = 0
    for size in sizes:
        piece = flat[start : start + size].reshape(n_place, size // n_place)
        gain_pieces.append(lax.dynamic_index_in_dim(piece, place, 0, keepdims=False))
        start += size
    gain_out = [
        jnp.stack([gain_pieces[4 * layer_idx + member] for layer_idx in range(layer_count)])
        for member in range(4)
    ]
    hidden_here = w_gate.shape[2]
    mlp_split = [split_columns(rows, [hidden_here] * 3) for rows in mlp_rows]
    attn_split = [
        split_columns(
            rows, [w_query.shape[2], key_weight.shape[2], value_weight.shape[2], w_out.shape[1]]
        )
        for rows in attn_rows
    ]
    return (
        turn(resid),
        turn(upstream),
        jnp.stack([pieces[0] for pieces in attn_split]),
        jnp.stack([pieces[1] for pieces in attn_split]),
        jnp.stack([pieces[2] for pieces in attn_split]),
        jnp.stack([pieces[3].T for pieces in attn_split]),
        jnp.stack([pieces[0] for pieces in mlp_split]),
        jnp.stack([pieces[1] for pieces in mlp_split]),
        jnp.stack([pieces[2].T for pieces in mlp_split]),
        gain_out[0],
        gain_out[1],
        gain_out[2],
        gain_out[3],
    )


def solution(mesh):
    fine = Mesh(
        mesh.devices.reshape(2, 4, 4, 2, 2), ("x_lo", "z", "y", "x_hi", "core")
    )
    dp = ("x_lo", "z", "y")
    tensor = ("x_hi", "core")
    return jax.shard_map(
        shards,
        mesh=fine,
        in_specs=(
            P(dp, None),
            P(dp, None),
            P(dp, None),
            P(None, None, tensor),
            P(None, None, tensor),
            P(None, None, tensor),
            P(None, tensor, None),
            P(None, None, tensor),
            P(None, None, tensor),
            P(None, tensor, None),
            P(),
            P(),
            P(),
            P(),
            P(dp, None),
        ),
        out_specs=(
            P(dp, None),
            P(dp, None),
            P(None, dp, tensor),
            P(None, dp, tensor),
            P(None, dp, tensor),
            P(None, tensor, dp),
            P(None, dp, tensor),
            P(None, dp, tensor),
            P(None, tensor, dp),
            P(None, dp),
            P(None, dp),
            P(None, dp),
            P(None, dp),
        ),
        check_vma=False,
    )
```

time: 2070 us -> 553 us (0.27)
  waiting for transfers between devices: 1780 us -> 324 us
  blocking collectives: 97.6 us -> 0 us
  starting transfers between devices: 1.6 us -> 48.3 us
  matrix products: 55.5 us -> 27.6 us
  Pallas kernels: 0 us -> 24.2 us
    reduce_scatter x13 -> x4, waiting for transfers between devices: 1100 us -> 184 us  [scatter_rows(): lax.psum_scatter(stacked, ('z', 'y'), scatter_dimension=0, tiled=True)]
    unnamed x27 -> x4, waiting for transfers between devices: 534 us -> 0.07 us
    all_gather x8 -> x0, waiting for transfers between devices: 142 us -> none  [the longest x2 43.3 us: layer_backward(): grad_mlp_in = lax.all_gather(mlp_back_share, 'tensor', axis=0, tiled=True)]
    ppermute x0 -> x35, waiting for transfers between devices: none -> 139 us  [the longest x8 96.7 us: group_sum(): own = own + lax.ppermute(own, 'x_hi', SWAP)]
    unnamed x3 -> x0, blocking collectives: 97.6 us -> none
    ppermute x0 -> x35, starting transfers between devices: none -> 48.1 us  [the longest x8 23.2 us: group_sum(): own = own + lax.ppermute(own, 'x_hi', SWAP)]
    pallas_call x0 -> x4, Pallas kernels: none -> 24.2 us  [weight_grads(): pl.pallas_call(body, grid=(2 * per_half,), in_specs=[pl.BlockSpec((tokens...]
  transfers between devices with their start and end apart: 24 -> 39, of which waited for: 24 -> 33; matrix products, arithmetic and copies ran while one was open for 4% -> 10% of each run, Pallas kernels for 0% -> 3%
where the time goes in v1:
time: 553 us; the launch traced here: 543 us
  waiting for transfers between devices  324 us (59%)
  local copies, waits for them, and re-layouts  56.1 us (10%)
  starting transfers between devices  48.3 us (9%)
  other arithmetic  47.3 us (9%)
  matrix products  27.6 us (5%)
  Pallas kernels  24.2 us (4%)
  between operations  16.3 us (3%)
    reduce_scatter x4, waiting for transfers between devices, scatter_rows(): lax.psum_scatter(stacked, ('z', 'y'), scatter_dimension=0, tiled=True)  184 us
    ppermute x8, waiting for transfers between devices, group_sum(): own = own + lax.ppermute(own, 'x_hi', SWAP)  96.7 us
    pallas_call x4, Pallas kernels, weight_grads(): pl.pallas_call(body, grid=(2 * per_half,), in_specs=[pl.BlockSpec((tokens...  24.2 us
    ppermute x8, starting transfers between devices, group_sum(): own = own + lax.ppermute(own, 'x_hi', SWAP)  23.2 us
    unnamed x271, local copies, waits for them, and re-layouts  18.9 us
    ppermute x4, waiting for transfers between devices, scatter_rows(): return keep + lax.ppermute(send, 'x_lo', SWAP)  12.9 us
    ppermute x5, starting transfers between devices, sum_everywhere(): lax.ppermute(small, axis, [(i, i ^ step) for i in range(size)])  12.1 us
  transfers between devices with their start and end apart: 39, of which 33 were waited for; matrix products, arithmetic and copies ran while one was open for 10% of the time, Pallas kernels for 3%

profile of v1, /device:TPU:0, one launch (start us, length us, event | category | flops | bytes accessed | tf_op | source)
XLA Modules:
  0.0 543.3 jit_solution(15207323941887495575)
XLA Ops:
  13.8 2.2 convolution_convert_fusion.5
  24.2 1.9 collective-permute-done
  26.2 3.2 collective-permute-start.1
  29.4 12.3 %collective-permute-done.1 = f32[128,1024]{1,0:T(8,128)S(1)} collective-permute-done((f32[128,1024]{1,0:T(8,128)S(1)}, f32[128,1024]{1,0:T(8,128)S(1)}, u32[]{:S(2)}, u32[]{:S(2)}) %collective-permute-start.1) | collective-permute-done | bytes 524320 | tf_op jit(solution)/shard_map/ppermute | solution.py:97
  49.7 1.7 collective-permute-done.3
  51.5 3.2 collective-permute-start.4
  54.7 12.5 %collective-permute-done.4 = f32[128,1024]{1,0:T(8,128)S(1)} collective-permute-done((f32[128,1024]{1,0:T(8,128)S(1)}, f32[128,1024]{1,0:T(8,128)S(1)}, u32[]{:S(2)}, u32[]{:S(2)}) %collective-permute-start.4) | collective-permute-done | bytes 524320 | tf_op jit(solution)/shard_map/ppermute | solution.py:97
  67.3 2.4 copy.70
  75.0 1.8 copy.72
  76.8 1.8 copy.71
  78.5 1.6 multiply_reduce_fusion.21
  85.8 3.2 collective-permute-start.7
  89.0 12.6 %collective-permute-done.7 = f32[128,1024]{1,0:T(8,128)S(1)} collective-permute-done((f32[128,1024]{1,0:T(8,128)S(1)}, f32[128,1024]{1,0:T(8,128)S(1)}, u32[]{:S(2)}, u32[]{:S(2)}) %collective-permute-start.7) | collective-permute-done | bytes 524320 | tf_op jit(solution)/shard_map/ppermute | solution.py:97
  110.8 3.2 collective-permute-start.13
  114.8 12.3 %collective-permute-done.13 = f32[128,1024]{1,0:T(8,128)S(1)} collective-permute-done((f32[128,1024]{1,0:T(8,128)S(1)}, f32[128,1024]{1,0:T(8,128)S(1)}, u32[]{:S(2)}, u32[]{:S(2)}) %collective-permute-start.13) | collective-permute-done | bytes 524320 | tf_op jit(solution)/shard_map/ppermute | solution.py:97
  128.0 9.5 %collective-permute-done.10 = f32[128,1024]{1,0:T(8,128)S(1)} collective-permute-done((f32[128,1024]{1,0:T(8,128)S(1)}, f32[128,1024]{1,0:T(8,128)S(1)}, u32[]{:S(2)}, u32[]{:S(2)}) %collective-permute-start.10) | collective-permute-done | bytes 524320 | tf_op jit(solution)/shard_map/ppermute | solution.py:97
  138.5 1.8 copy.135.refs_5_
  140.3 2.9 multiply_reduce_fusion
  143.3 3.4 fusion.120
  148.6 1.7 reshape.421
  150.4 1.8 copy.83
  152.2 2.0 bitcast_convert_fusion.1
  154.1 2.1 copy.108
  157.5 1.9 fusion.57
  164.3 1.8 copy.138.refs_2_
  166.1 1.7 copy.139.refs_3_
  167.8 1.7 copy.140.refs_4_
  169.4 5.5 %weight_grads.5 = f32[16,2,32,1536]{3,2,1,0:T(8,128)} custom-call(bf16[256,1024]{1,0:T(8,128)(2,1)} %copy-done.13, bf16[256,1024]{1,0:T(8,128)(2,1)} %copy-done.51, bf16[256,512]{1,0:T(8,128)(2,1)} %copy.138.refs_2_, bf16[256,256]{1,0:T(8,128)(2,1)} %copy.139.refs_3_, bf16[256,256]{1,0:T(8,128)(2,1)} %copy.140.refs_4_, bf16[256,512]{1,0:T(8,128)(2,1)} %copy.135.refs_5_), custom_call_target="tpu_custom_call" | custom-call | flops 805306368 | bytes 6291456 | tf_op jit(solution)/shard_map/weight_grads/pallas_call | solution.py:134
  175.1 1.9 fusion.70
  180.0 3.4 collective-permute-start.16
  183.4 12.6 %collective-permute-done.16 = f32[128,1024]{1,0:T(8,128)S(1)} collective-permute-done((f32[128,1024]{1,0:T(8,128)S(1)}, f32[128,1024]{1,0:T(8,128)S(1)}, u32[]{:S(2)}, u32[]{:S(2)}) %collective-permute-start.16) | collective-permute-done | bytes 524320 | tf_op jit(solution)/shard_map/ppermute | solution.py:97
  196.2 1.9 collective-permute-done.17
  205.7 1.7 collective-permute-done.18
  207.5 3.2 collective-permute-start.19
  210.7 12.4 %collective-permute-done.19 = f32[128,1024]{1,0:T(8,128)S(1)} collective-permute-done((f32[128,1024]{1,0:T(8,128)S(1)}, f32[128,1024]{1,0:T(8,128)S(1)}, u32[]{:S(2)}, u32[]{:S(2)}) %collective-permute-start.19) | collective-permute-done | bytes 524320 | tf_op jit(solution)/shard_map/ppermute | solution.py:97
  224.0 1.8 copy.132.refs_5_
  226.2 2.2 multiply_reduce_fusion.2
  228.4 1.7 fusion.118
  232.7 2.1 copy.122
  238.4 1.8 copy.143.refs_2_
  244.6 5.5 %weight_grads.4 = f32[16,2,32,1536]{3,2,1,0:T(8,128)} custom-call(bf16[256,1024]{1,0:T(8,128)(2,1)} %copy-done.8, bf16[256,1024]{1,0:T(8,128)(2,1)} %copy-done.52, bf16[256,512]{1,0:T(8,128)(2,1)} %copy.143.refs_2_, bf16[256,256]{1,0:T(8,128)(2,1)} %copy.144.refs_3_, bf16[256,256]{1,0:T(8,128)(2,1)} %copy.145.refs_4_, bf16[256,512]{1,0:T(8,128)(2,1)} %copy.132.refs_5_), custom_call_target="tpu_custom_call" | custom-call | flops 805306368 | bytes 6291456 | tf_op jit(solution)/shard_map/weight_grads/pallas_call | solution.py:134
  250.2 6.7 %weight_grads.7 = f32[16,2,32,2304]{3,2,1,0:T(8,128)} custom-call(bf16[256,1024]{1,0:T(8,128)(2,1)} %copy-done.59, bf16[256,1024]{1,0:T(8,128)(2,1)} %copy-done.16, bf16[256,768]{1,0:T(8,128)(2,1)} %copy-done.68, bf16[256,768]{1,0:T(8,128)(2,1)} %copy-done.66, bf16[256,768]{1,0:T(8,128)(2,1)} %copy-done.65), custom_call_target="tpu_custom_call" | custom-call | flops 1207959552 | bytes 9437184 | tf_op jit(solution)/shard_map/weight_grads/pallas_call | solution.py:134
  257.0 6.6 %weight_grads.6 = f32[16,2,32,2304]{3,2,1,0:T(8,128)} custom-call(bf16[256,1024]{1,0:T(8,128)(2,1)} %copy-done.58, bf16[256,1024]{1,0:T(8,128)(2,1)} %copy-done.50, bf16[256,768]{1,0:T(8,128)(2,1)} %copy-done.69, bf16[256,768]{1,0:T(8,128)(2,1)} %copy-done.67, bf16[256,768]{1,0:T(8,128)(2,1)} %copy-done.64), custom_call_target="tpu_custom_call" | custom-call | flops 1207959552 | bytes 9437184 | tf_op jit(solution)/shard_map/weight_grads/pallas_call | solution.py:134
  263.6 1.6 copy-done.10
  267.4 1.7 collective-permute-done.21
  269.3 3.1 collective-permute-start.22
  272.5 12.5 %collective-permute-done.22 = f32[128,1024]{1,0:T(8,128)S(1)} collective-permute-done((f32[128,1024]{1,0:T(8,128)S(1)}, f32[128,1024]{1,0:T(8,128)S(1)}, u32[]{:S(2)}, u32[]{:S(2)}) %collective-permute-start.22) | collective-permute-done | bytes 524320 | tf_op jit(solution)/shard_map/ppermute | solution.py:97
  285.1 1.9 collective-permute-done.23
  287.9 1.6 collective-permute-start.28
  289.6 2.2 collective-permute-done.28
  291.8 1.8 collective-permute-start.29
  293.7 2.5 collective-permute-done.29
  296.2 3.0 collective-permute-start.30
  303.2 2.3 collective-permute-done.31
  305.5 4.1 collective-permute-start.32
  312.7 3.0 collective-permute-start.34
  321.5 1.7 collective-permute-start.25
  323.8 3.9 collective-permute-done.25
  328.7 15.9 %reduce-scatter.5.cloned.1.call-done = f32[64,1536]{1,0:T(8,128)} async-done(((f32[1024,1536]{1,0:T(8,128)}), f32[64,1536]{1,0:T(8,128)}) %reduce-scatter.5.cloned.1.call-update) | async-done | bytes 393232 | tf_op jit(solution)/shard_map/reduce_scatter | solution.py:152
  345.5 1.6 collective-permute-start.24
  347.1 4.2 collective-permute-done.24
  354.9 80.4 %reduce-scatter.11.cloned.1.call-done = f32[64,2304]{1,0:T(8,128)} async-done(((f32[1024,2304]{1,0:T(8,128)}), f32[64,2304]{1,0:T(8,128)}) %reduce-scatter.11.cloned.1.call-update) | async-done | bytes 589840 | tf_op jit(solution)/shard_map/reduce_scatter | solution.py:152
  437.8 88.1 %reduce-scatter.9.cloned.1.call-done = f32[64,2304]{1,0:T(8,128)} async-done(((f32[1024,2304]{1,0:T(8,128)}), f32[64,2304]{1,0:T(8,128)}) %reduce-scatter.9.cloned.1.call-update) | async-done | bytes 589840 | tf_op jit(solution)/shard_map/reduce_scatter | solution.py:152
  529.5 4.9 collective-permute-done.26
  (513 shorter events, 106.1 us)
Async XLA Ops:
  7.2 313.4 %reduce-scatter.7.cloned.1.call-start = ((), (), s32[]{:S(2)}) async-start(), calls=%async_computation.5 | async-start | bytes 6684672 | tf_op jit(solution)/shard_map/reduce_scatter | solution.py:152
  9.3 62.9 %copy-start.91 = (f32[1,1024]{1,0:T(1,128)}, f32[1,1024]{1,0:T(1,128)S(1)}, u32[]{:S(2)}) copy-start(f32[1,1024]{1,0:T(1,128)S(1)} %get-tuple-element.101) | copy-start | bytes 12292
  10.6 33.3 %copy-start.4 = (bf16[256,1024]{1,0:T(8,128)(2,1)}, bf16[256,1024]{1,0:T(8,128)(2,1)S(1)}, u32[]{:S(2)}) copy-start(bf16[256,1024]{1,0:T(8,128)(2,1)S(1)} %get-tuple-element.46) | copy-start | bytes 1572868
  13.8 6.6 %copy-start.8 = (bf16[256,1024]{1,0:T(8,128)(2,1)}, bf16[256,1024]{1,0:T(8,128)(2,1)S(1)}, u32[]{:S(2)}) copy-start(bf16[256,1024]{1,0:T(8,128)(2,1)S(1)} %fusion.60.refs_0_) | copy-start | bytes 1572868
  24.1 17.9 %copy-start.118 = (f32[2,1024]{1,0:T(2,128)S(1)}, f32[2,1024]{1,0:T(2,128)}, u32[]{:S(2)}) copy-start(f32[2,1024]{1,0:T(2,128)} %param.26) | copy-start | bytes 24580
  24.1 2.0 collective-permute-start
  26.2 15.5 %collective-permute-start.1 = (f32[128,1024]{1,0:T(8,128)S(1)}, f32[128,1024]{1,0:T(8,128)S(1)}, u32[]{:S(2)}, u32[]{:S(2)}) collective-permute-start(f32[128,1024]{1,0:T(8,128)S(1)} %slice_add_fusion.7), channel_id=1, source_target_pairs={{0,2},{2,0},{1,3},{3,1},{4,6},{6,4},{5,7},{7,5},{8,10},{10,8},{9,1... | collective-permute-start | bytes 1572872 | tf_op jit(solution)/shard_map/ppermute | solution.py:97
  41.8 2.0 collective-permute-start.2
  49.4 2.0 collective-permute-start.3
  51.5 18.2 %copy-start.61 = (bf16[256,1024]{0,1:T(8,128)(2,1)S(1)}, bf16[256,1024]{0,1:T(8,128)(2,1)}, u32[]{:S(2)}) copy-start(bf16[256,1024]{0,1:T(8,128)(2,1)} %get-tuple-element.59) | copy-start | bytes 1572868
  51.5 15.7 %collective-permute-start.4 = (f32[128,1024]{1,0:T(8,128)S(1)}, f32[128,1024]{1,0:T(8,128)S(1)}, u32[]{:S(2)}, u32[]{:S(2)}) collective-permute-start(f32[128,1024]{1,0:T(8,128)S(1)} %slice_add_fusion.6), channel_id=1, source_target_pairs={{0,2},{2,0},{1,3},{3,1},{4,6},{6,4},{5,7},{7,5},{8,10},{10,8},{9,1... | collective-permute-start | bytes 1572872 | tf_op jit(solution)/shard_map/ppermute | solution.py:97
  67.2 3.5 collective-permute-start.5
  82.9 6.1 %copy-start.57 = (bf16[256,1024]{1,0:T(8,128)(2,1)S(1)}, bf16[256,1024]{1,0:T(8,128)(2,1)}, u32[]{:S(2)}) copy-start(bf16[256,1024]{1,0:T(8,128)(2,1)} %param.29) | copy-start | bytes 1572868
  83.4 2.4 collective-permute-start.6
  85.8 16.2 %copy-start.30 = (bf16[2,768,1024]{2,1,0:T(8,128)(2,1)S(1)}, bf16[2,768,1024]{2,1,0:T(8,128)(2,1)}, u32[]{:S(2)}) copy-start(bf16[2,768,1024]{2,1,0:T(8,128)(2,1)} %param.24) | copy-start | bytes 9437188
  85.8 15.8 %collective-permute-start.7 = (f32[128,1024]{1,0:T(8,128)S(1)}, f32[128,1024]{1,0:T(8,128)S(1)}, u32[]{:S(2)}, u32[]{:S(2)}) collective-permute-start(f32[128,1024]{1,0:T(8,128)S(1)} %slice_add_fusion.5), channel_id=1, source_target_pairs={{0,2},{2,0},{1,3},{3,1},{4,6},{6,4},{5,7},{7,5},{8,10},{10,8},{9,1... | collective-permute-start | bytes 1572872 | tf_op jit(solution)/shard_map/ppermute | solution.py:97
  101.7 2.0 collective-permute-start.8
  108.7 2.0 collective-permute-start.12
  109.5 4.5 collective-permute-start.9
  110.8 16.4 %collective-permute-start.13 = (f32[128,1024]{1,0:T(8,128)S(1)}, f32[128,1024]{1,0:T(8,128)S(1)}, u32[]{:S(2)}, u32[]{:S(2)}) collective-permute-start(f32[128,1024]{1,0:T(8,128)S(1)} %slice_add_fusion.3), channel_id=1, source_target_pairs={{0,2},{2,0},{1,3},{3,1},{4,6},{6,4},{5,7},{7,5},{8,10},{10,8},{9,1... | collective-permute-start | bytes 1572872 | tf_op jit(solution)/shard_map/ppermute | solution.py:97
  114.1 23.5 %collective-permute-start.10 = (f32[128,1024]{1,0:T(8,128)S(1)}, f32[128,1024]{1,0:T(8,128)S(1)}, u32[]{:S(2)}, u32[]{:S(2)}) collective-permute-start(f32[128,1024]{1,0:T(8,128)S(1)} %slice_add_fusion.4), channel_id=1, source_target_pairs={{0,2},{2,0},{1,3},{3,1},{4,6},{6,4},{5,7},{7,5},{8,10},{10,8},{9,1... | collective-permute-start | bytes 1572872 | tf_op jit(solution)/shard_map/ppermute | solution.py:97
  128.0 12.3 %collective-permute-start.14 = (f32[128,1024]{1,0:T(8,128)}, f32[128,1024]{1,0:T(8,128)}, u32[]{:S(2)}, u32[]{:S(2)}) collective-permute-start(f32[128,1024]{1,0:T(8,128)} %add.314), channel_id=1, source_target_pairs={{0,1},{1,0},{2,3},{3,2},{4,5},{5,4},{6,7},{7,6},{8,9},{9,8},{10,11... | collective-permute-start | bytes 1572872 | tf_op jit(solution)/shard_map/ppermute | solution.py:98
  138.5 4.7 collective-permute-start.11
  175.0 169.6 %reduce-scatter.5.cloned.1.call-start = ((), (), s32[]{:S(2)}) async-start(), calls=%async_computation.4 | async-start | bytes 6684672 | tf_op jit(solution)/shard_map/reduce_scatter | solution.py:152
  177.8 20.3 %copy-start.92 = (f32[1,1024]{1,0:T(1,128)S(1)}, f32[1,1024]{1,0:T(1,128)}, u32[]{:S(2)}) copy-start(f32[1,1024]{1,0:T(1,128)} %copy-done.91) | copy-start | bytes 12292
  177.8 20.3 %copy-start.108 = (f32[256]{0:T(256)S(1)}, f32[256]{0:T(256)}, u32[]{:S(2)}) copy-start(f32[256]{0:T(256)} %copy-done.107) | copy-start | bytes 3076
  177.8 2.1 collective-permute-start.15
  180.0 18.4 %copy-start.18 = (f32[256,1024]{1,0:T(8,128)S(1)}, f32[256,1024]{1,0:T(8,128)}, u32[]{:S(2)}) copy-start(f32[256,1024]{1,0:T(8,128)} %get-tuple-element.38) | copy-start | bytes 3145732
  180.0 16.0 %collective-permute-start.16 = (f32[128,1024]{1,0:T(8,128)S(1)}, f32[128,1024]{1,0:T(8,128)S(1)}, u32[]{:S(2)}, u32[]{:S(2)}) collective-permute-start(f32[128,1024]{1,0:T(8,128)S(1)} %slice_add_fusion.2), channel_id=1, source_target_pairs={{0,2},{2,0},{1,3},{3,1},{4,6},{6,4},{5,7},{7,5},{8,10},{10,8},{9,1... | collective-permute-start | bytes 1572872 | tf_op jit(solution)/shard_map/ppermute | solution.py:97
  196.1 2.0 collective-permute-start.17
  205.4 20.8 %copy-start.94 = (f32[1,1024]{1,0:T(1,128)S(1)}, f32[1,1024]{1,0:T(1,128)}, u32[]{:S(2)}) copy-start(f32[1,1024]{1,0:T(1,128)} %copy-done.93) | copy-start | bytes 12292
  205.4 2.0 collective-permute-start.18
  207.5 15.6 %collective-permute-start.19 = (f32[128,1024]{1,0:T(8,128)S(1)}, f32[128,1024]{1,0:T(8,128)S(1)}, u32[]{:S(2)}, u32[]{:S(2)}) collective-permute-start(f32[128,1024]{1,0:T(8,128)S(1)} %slice_add_fusion.1), channel_id=1, source_target_pairs={{0,2},{2,0},{1,3},{3,1},{4,6},{6,4},{5,7},{7,5},{8,10},{10,8},{9,1... | collective-permute-start | bytes 1572872 | tf_op jit(solution)/shard_map/ppermute | solution.py:97
  224.0 2.3 collective-permute-start.20
  231.7 4.6 copy-start.47
  242.8 7.4 %copy-start.70 = (bf16[256,2,128]{0,2,1:T(8,128)(2,1)}, bf16[256,2,128]{0,2,1:T(8,128)(2,1)S(1)}, u32[]{:S(2)}) copy-start(bf16[256,2,128]{0,2,1:T(8,128)(2,1)S(1)} %multiply_convert_fusion.11) | copy-start | bytes 393220
  250.2 185.2 %reduce-scatter.11.cloned.1.call-start = ((), (), s32[]{:S(2)}) async-start(), calls=%async_computation.7 | async-start | bytes 10027008 | tf_op jit(solution)/shard_map/reduce_scatter | solution.py:152
  256.9 269.0 %reduce-scatter.9.cloned.1.call-start = ((), (), s32[]{:S(2)}) async-start(), calls=%async_computation.6 | async-start | bytes 10027008 | tf_op jit(solution)/shard_map/reduce_scatter | solution.py:152
  267.1 19.9 %copy-start.5 = (bf16[256,1024]{1,0:T(8,128)(2,1)S(1)}, bf16[256,1024]{1,0:T(8,128)(2,1)}, u32[]{:S(2)}) copy-start(bf16[256,1024]{1,0:T(8,128)(2,1)} %copy-done.4) | copy-start | bytes 1572868
  267.1 19.9 %copy-start.98 = (f32[1,1024]{1,0:T(1,128)S(1)}, f32[1,1024]{1,0:T(1,128)}, u32[]{:S(2)}) copy-start(f32[1,1024]{1,0:T(1,128)} %copy-done.97) | copy-start | bytes 12292
  267.1 19.9 %copy-start.112 = (f32[256]{0:T(256)S(1)}, f32[256]{0:T(256)}, u32[]{:S(2)}) copy-start(f32[256]{0:T(256)} %copy-done.111) | copy-start | bytes 3076
  267.2 2.0 collective-permute-start.21
  269.3 18.6 %copy-start.104 = (f32[1024]{0:T(1024)S(1)}, f32[1024]{0:T(1024)}, u32[]{:S(2)}) copy-start(f32[1024]{0:T(1024)} %get-tuple-element.21) | copy-start | bytes 12292
  269.3 18.5 %copy-start.125 = (f32[128]{0:T(128)S(1)}, f32[128]{0:T(128)}, u32[]{:S(2)}) copy-start(f32[128]{0:T(128)} %get-tuple-element.15) | copy-start | bytes 1540
  269.3 18.6 %copy-start.127 = (f32[128]{0:T(128)S(1)}, f32[128]{0:T(128)}, u32[]{:S(2)}) copy-start(f32[128]{0:T(128)} %get-tuple-element.25) | copy-start | bytes 1540
  269.3 18.6 %copy-start.103 = (f32[1024]{0:T(1024)S(1)}, f32[1024]{0:T(1024)}, u32[]{:S(2)}) copy-start(f32[1024]{0:T(1024)} %get-tuple-element.17) | copy-start | bytes 12292
  269.3 18.6 %copy-start.124 = (f32[128]{0:T(128)S(1)}, f32[128]{0:T(128)}, u32[]{:S(2)}) copy-start(f32[128]{0:T(128)} %get-tuple-element.13) | copy-start | bytes 1540
  269.3 18.6 %copy-start.126 = (f32[128]{0:T(128)S(1)}, f32[128]{0:T(128)}, u32[]{:S(2)}) copy-start(f32[128]{0:T(128)} %get-tuple-element.23) | copy-start | bytes 1540
  269.3 24.3 %copy-start.6 = (f32[256,1024]{1,0:T(8,128)S(1)}, f32[256,1024]{1,0:T(8,128)}, u32[]{:S(2)}) copy-start(f32[256,1024]{1,0:T(8,128)} %get-tuple-element.56) | copy-start | bytes 3145732
  269.3 15.6 %collective-permute-start.22 = (f32[128,1024]{1,0:T(8,128)S(1)}, f32[128,1024]{1,0:T(8,128)S(1)}, u32[]{:S(2)}, u32[]{:S(2)}) collective-permute-start(f32[128,1024]{1,0:T(8,128)S(1)} %slice_add_fusion), channel_id=1, source_target_pairs={{0,2},{2,0},{1,3},{3,1},{4,6},{6,4},{5,7},{7,5},{8,10},{10,8},{9,1... | collective-permute-start | bytes 1572872 | tf_op jit(solution)/shard_map/ppermute | solution.py:97
  285.0 2.0 collective-permute-start.23
  287.9 3.9 collective-permute-start.28
  291.8 4.4 collective-permute-start.29
  293.7 16.0 %copy-start.63 = (f32[128,1024]{1,0:T(8,128)S(1)}, f32[128,1024]{1,0:T(8,128)}, u32[]{:S(2)}) copy-start(f32[128,1024]{1,0:T(8,128)} %copy-done.62) | copy-start | bytes 1572868
  296.2 5.5 %collective-permute-start.30 = (f32[36,128]{1,0:T(8,128)S(1)}, f32[36,128]{1,0:T(8,128)S(1)}, u32[]{:S(2)}, u32[]{:S(2)}) collective-permute-start(f32[36,128]{1,0:T(8,128)S(1)} %fusion.171), channel_id=1, source_target_pairs={{0,8},{4,12},{8,0},{12,4},{1,9},{5,13},{9,1},{13,5},{2,10},{6,14},... | collective-permute-start | bytes 55304 | tf_op jit(solution)/shard_map/ppermute | solution.py:166
  301.7 3.8 collective-permute-start.31
  305.5 6.0 %collective-permute-start.32 = (f32[36,128]{1,0:T(8,128)S(1)}, f32[36,128]{1,0:T(8,128)S(1)}, u32[]{:S(2)}, u32[]{:S(2)}) collective-permute-start(f32[36,128]{1,0:T(8,128)S(1)} %add.344), channel_id=1, source_target_pairs={{0,32},{16,48},{32,0},{48,16},{1,33},{17,49},{33,1},{49,17},{2,34}... | collective-permute-start | bytes 55304 | tf_op jit(solution)/shard_map/ppermute | solution.py:166
  311.5 1.2 collective-permute-start.33
  312.7 5.3 collective-permute-start.34
  321.5 6.2 %collective-permute-start.25 = (f32[32,1536]{1,0:T(8,128)S(1)}, f32[32,1536]{1,0:T(8,128)S(1)}, u32[]{:S(2)}, u32[]{:S(2)}) collective-permute-start(f32[32,1536]{1,0:T(8,128)S(1)} %dynamic-slice_bitcast_fusion.2), channel_id=1, source_target_pairs={{0,64},{64,0},{1,65},{65,1},{2,66},{66,2},{3,67},{67,3},{4,68},{68... | collective-permute-start | bytes 589832 | tf_op jit(solution)/shard_map/ppermute | solution.py:158
  345.5 5.7 %collective-permute-start.24 = (f32[32,1536]{1,0:T(8,128)S(1)}, f32[32,1536]{1,0:T(8,128)S(1)}, u32[]{:S(2)}, u32[]{:S(2)}) collective-permute-start(f32[32,1536]{1,0:T(8,128)S(1)} %dynamic-slice_bitcast_fusion.3), channel_id=1, source_target_pairs={{0,64},{64,0},{1,65},{65,1},{2,66},{66,2},{3,67},{67,3},{4,68},{68... | collective-permute-start | bytes 589832 | tf_op jit(solution)/shard_map/ppermute | solution.py:158
  436.3 92.2 %collective-permute-start.27 = (f32[32,2304]{1,0:T(8,128)S(1)}, f32[32,2304]{1,0:T(8,128)S(1)}, u32[]{:S(2)}, u32[]{:S(2)}) collective-permute-start(f32[32,2304]{1,0:T(8,128)S(1)} %dynamic-slice_bitcast_fusion), channel_id=1, source_target_pairs={{0,64},{64,0},{1,65},{65,1},{2,66},{66,2},{3,67},{67,3},{4,68},{68... | collective-permute-start | bytes 884744 | tf_op jit(solution)/shard_map/ppermute | solution.py:158
  525.9 8.5 %copy-start.87 = (f32[64,2304]{1,0:T(8,128)S(1)}, f32[64,2304]{1,0:T(8,128)}, u32[]{:S(2)}) copy-start(f32[64,2304]{1,0:T(8,128)} %reduce-scatter.9.cloned.1.call-done) | copy-start | bytes 1769476
  527.0 7.4 %collective-permute-start.26 = (f32[32,2304]{1,0:T(8,128)S(1)}, f32[32,2304]{1,0:T(8,128)S(1)}, u32[]{:S(2)}, u32[]{:S(2)}) collective-permute-start(f32[32,2304]{1,0:T(8,128)S(1)} %dynamic-slice_bitcast_fusion.1), channel_id=1, source_target_pairs={{0,64},{64,0},{1,65},{65,1},{2,66},{66,2},{3,67},{67,3},{4,68},{68... | collective-permute-start | bytes 884744 | tf_op jit(solution)/shard_map/ppermute | solution.py:158
  (106 other events, 237.0 us)
Sparse Core Ops, SparseCore 0:
  175.1 84.5 reduce-scatter.6
  263.1 81.4 reduce-scatter.4
  348.1 87.1 reduce-scatter.10
  438.7 87.2 reduce-scatter.8

commit v2 on v1

--- a/solution.py
+++ b/solution.py
@@ -91,11 +91,17 @@
     return (grad_queries, grad_keys, grad_values)
 
 
-def group_sum(partial):
+def group_sum(partial, beside=None):
     half = partial.shape[0] // 2
     own = partial[:half] + lax.ppermute(partial[half:], "core", SWAP)
-    own = own + lax.ppermute(own, "x_hi", SWAP)
-    return jnp.concatenate([own, lax.ppermute(own, "core", SWAP)], axis=0)
+    other = lax.ppermute(own, "x_hi", SWAP)
+    made = None
+    if beside is not None:
+        made = beside()
+        other, made = lax.optimization_barrier((other, made))
+    own = own + other
+    total = jnp.concatenate([own, lax.ppermute(own, "core", SWAP)], axis=0)
+    return total if beside is None else (total, made)
 
 
 def weight_grads(pairs):
@@ -148,14 +154,47 @@
     return out.reshape(width, total)
 
 
-def scatter_rows(stacked):
-    part = lax.psum_scatter(stacked, ("z", "y"), scatter_dimension=0, tiled=True)
+def swap_partner_rows(part):
     rows = part.shape[0] // 2
     part = part.reshape(2, rows, part.shape[1])
     mine = lax.axis_index("x_lo")
     keep = lax.dynamic_index_in_dim(part, mine, 0, keepdims=False)
     send = lax.dynamic_index_in_dim(part, 1 - mine, 0, keepdims=False)
     return keep + lax.ppermute(send, "x_lo", SWAP)
+
+
+def scatter_zy(stacked):
+    return lax.psum_scatter(stacked, ("z", "y"), scatter_dimension=0, tiled=True)
+
+
+def ring_scatter(block, dim, axis):
+    up = [(i, (i + 1) % 4) for i in range(4)]
+    down = [(i, (i - 1) % 4) for i in range(4)]
+    mine = lax.axis_index(axis)
+
+    def entry(offset):
+        return lax.dynamic_index_in_dim(block, (mine + offset) % 4, dim, keepdims=False)
+
+    far, after, before, own = (entry(2), entry(1), entry(3), entry(0))
+    half = far.shape[0] // 2
+    far_up = lax.ppermute(far[:half], axis, up)
+    far_down = lax.ppermute(far[half:], axis, down)
+    near_up = lax.ppermute(after[half:], axis, up)
+    near_down = lax.ppermute(before[:half], axis, down)
+    last_up = lax.ppermute(after[:half] + far_up, axis, up)
+    last_down = lax.ppermute(before[half:] + far_down, axis, down)
+    return jnp.concatenate(
+        [own[:half] + near_down + last_up, own[half:] + near_up + last_down], axis=0
+    )
+
+
+def scatter_by_rings(stacked):
+    width, columns = stacked.shape
+    cut = columns // 2
+    block = stacked.reshape(4, 4, width // 16, columns)
+    first = ring_scatter(ring_scatter(block[..., :cut], 1, "y"), 0, "z")
+    second = ring_scatter(ring_scatter(block[..., cut:], 0, "z"), 0, "y")
+    return jnp.concatenate([first, second], axis=1)
 
 
 def sum_everywhere(small):
@@ -170,7 +209,7 @@
     return small
 
 
-def layer_forward(resid, allowed, cosine, sine, params):
+def layer_forward(resid, allowed, cosine, sine, params, last):
     (w_query, key_weight, value_weight, w_out, w_gate, w_up, w_down) = params[:7]
     (gain_in, gain_post, gain_query, gain_key) = params[7:]
     length = resid.shape[0]
@@ -204,8 +243,8 @@
     gate_logits = jnp.dot(mlp_input, w_gate, preferred_element_type=jnp.float32)
     up_pre = jnp.dot(mlp_input, w_up, preferred_element_type=jnp.float32)
     hidden = (jax.nn.silu(gate_logits) * up_pre).astype(jnp.bfloat16)
-    mlp_sum = group_sum(jnp.dot(hidden, w_down, preferred_element_type=jnp.float32))
-    result = middle + mlp_sum
+    mlp_partial = jnp.dot(hidden, w_down, preferred_element_type=jnp.float32)
+    result = (middle, mlp_partial) if last else middle + group_sum(mlp_partial)
     saved = (
         scale_in,
         normed_in,
@@ -229,7 +268,7 @@
     return (result, saved)
 
 
-def layer_backward(upstream, saved, params, allowed, cosine, sine):
+def layer_backward(upstream, saved, params, allowed, cosine, sine, carried, first):
     (w_query, key_weight, value_weight, w_out, w_gate, w_up, w_down) = params[:7]
     (gain_in, gain_post, gain_query, gain_key) = params[7:]
     (
@@ -263,12 +302,9 @@
     mlp_partial = jnp.dot(grad_gate_pre, w_gate.T, preferred_element_type=jnp.float32) + jnp.dot(
         grad_up_pre, w_up.T, preferred_element_type=jnp.float32
     )
-    grad_mlp_in = group_sum(mlp_partial)
-    mlp_grads = scatter_rows(
-        weight_grads(
-            [(mlp_input, grad_gate_pre), (mlp_input, grad_up_pre), (upstream_bf, hidden)]
-        )
-    )
+    mlp_pairs = [(mlp_input, grad_gate_pre), (mlp_input, grad_up_pre), (upstream_bf, hidden)]
+    grad_mlp_in, mlp_grads = group_sum(mlp_partial, lambda: weight_grads(carried + mlp_pairs))
+    mlp_grads = scatter_zy(mlp_grads)
     grad_gain_post = jnp.sum(mlp_partial * normed_post, axis=0)
     grad_middle = upstream + norm_back(grad_mlp_in, normed_post, scale_post, gain_post)
     middle_bf = grad_middle.astype(jnp.bfloat16)
@@ -298,21 +334,21 @@
         + jnp.dot(grad_keys, key_weight.T, preferred_element_type=jnp.float32)
         + jnp.dot(grad_values, value_weight.T, preferred_element_type=jnp.float32)
     )
-    attn_grads = scatter_rows(
-        weight_grads(
-            [
-                (attn_input, grad_queries),
-                (attn_input, grad_keys),
-                (attn_input, grad_values),
-                (middle_bf, attended),
-            ]
-        )
-    )
+    attn_pairs = [
+        (attn_input, grad_queries),
+        (attn_input, grad_keys),
+        (attn_input, grad_values),
+        (middle_bf, attended),
+    ]
+    if first:
+        made = weight_grads(attn_pairs)
+        attn_partial, made = lax.optimization_barrier((attn_partial, made))
+        attn_pairs = scatter_by_rings(made)
     grad_attn_in = group_sum(attn_partial)
     grad_gain_in = jnp.sum(attn_partial * normed_in, axis=0)
     grad_resid = grad_middle + norm_back(grad_attn_in, normed_in, scale_in, gain_in)
     gains = (grad_gain_in, grad_gain_post, query_gain_part, key_gain_part)
-    return (grad_resid, mlp_grads, attn_grads, gains)
+    return (grad_resid, mlp_grads, attn_pairs, attn_partial, gains)
 
 
 def split_columns(stacked, sizes):
@@ -373,18 +409,25 @@
     saves = []
     for layer_idx in range(layer_count):
         params = tuple((member[layer_idx] for member in all_params))
-        resid, saved = layer_forward(resid, allowed, cosine, sine, params)
+        resid, saved = layer_forward(
+            resid, allowed, cosine, sine, params, layer_idx == layer_count - 1
+        )
         saves.append(saved)
+    middle, last_partial = resid
     upstream = turn(cotangent).astype(jnp.float32)
-    mlp_rows, attn_rows, gains = ([], [], [])
+    scattered, gains, carried = ([], [], [])
     for layer_idx in reversed(range(layer_count)):
         params = tuple((member[layer_idx] for member in all_params))
-        upstream, mlp_part, attn_part, gain_part = layer_backward(
-            upstream, saves[layer_idx], params, allowed, cosine, sine
+        upstream, mlp_part, attn_part, attn_partial, gain_part = layer_backward(
+            upstream, saves[layer_idx], params, allowed, cosine, sine, carried, layer_idx == 0
         )
-        mlp_rows.insert(0, mlp_part)
-        attn_rows.insert(0, attn_part)
+        scattered.append(mlp_part)
+        carried = attn_part
         gains.insert(0, gain_part)
+    scattered.append(attn_part)
+    last_partial, _ = lax.optimization_barrier((last_partial, attn_partial))
+    resid = middle + group_sum(last_partial)
+    scattered = [swap_partner_rows(part) for part in scattered]
     sizes = [member.shape[1] for group in gains for member in [g[None] for g in group]]
     flat = sum_everywhere(
         jnp.concatenate([member for group in gains for member in group]).reshape(-1, 128)
@@ -401,14 +444,16 @@
         jnp.stack([gain_pieces[4 * layer_idx + member] for layer_idx in range(layer_count)])
         for member in range(4)
     ]
-    hidden_here = w_gate.shape[2]
-    mlp_split = [split_columns(rows, [hidden_here] * 3) for rows in mlp_rows]
-    attn_split = [
-        split_columns(
-            rows, [w_query.shape[2], key_weight.shape[2], value_weight.shape[2], w_out.shape[1]]
-        )
-        for rows in attn_rows
-    ]
+    mlp_sizes = [w_gate.shape[2], w_up.shape[2], w_down.shape[1]]
+    attn_sizes = [w_query.shape[2], key_weight.shape[2], value_weight.shape[2], w_out.shape[1]]
+    attn_split, mlp_split = ([], [])
+    for step, rows in enumerate(scattered):
+        sizes = (attn_sizes if step else []) + (mlp_sizes if step < layer_count else [])
+        pieces = split_columns(rows, sizes)
+        if step:
+            attn_split.insert(0, pieces[:4])
+        if step < layer_count:
+            mlp_split.insert(0, pieces[-3:])
     return (
         turn(resid),
         turn(upstream),

time: 553 us -> 445 us (0.80)
  waiting for transfers between devices: 324 us -> 190 us
  starting transfers between devices: 48.3 us -> 67.9 us
  matrix products: 27.6 us -> 35.6 us
    reduce_scatter x4 -> x2, waiting for transfers between devices: 184 us -> 0.01 us  [scatter_zy(): lax.psum_scatter(stacked, ('z', 'y'), scatter_dimension=0, tiled=True)]
    ppermute x20 -> x43, waiting for transfers between devices: 116 us -> 160 us  [the longest x8 60.6 us: group_sum(): other = lax.ppermute(own, 'x_hi', SWAP)]
    ppermute x20 -> x43, starting transfers between devices: 30 us -> 59 us  [the longest x8 21.8 us: group_sum(): other = lax.ppermute(own, 'x_hi', SWAP)]
    ppermute x5, starting transfers between devices: 12.1 us -> 3.26 us  [sum_everywhere(): lax.ppermute(small, axis, [(i, i ^ step) for i in range(size)])]
    ppermute x5, waiting for transfers between devices: 9.92 us -> 16.9 us  [sum_everywhere(): lax.ppermute(small, axis, [(i, i ^ step) for i in range(size)])]
    dot_general x12, matrix products: 6.51 us -> 12.8 us  [contract(): return jnp.einsum(form, left, right, preferred_element_type=jnp.float32)]
    unnamed x271 -> x259, local copies, waits for them, and re-layouts: 18.9 us -> 13.6 us
    pallas_call x4 -> x3, Pallas kernels: 24.2 us -> 21.2 us  [weight_grads(): pl.pallas_call(body, grid=(2 * per_half,), in_specs=[pl.BlockSpec((tokens...]
  transfers between devices with their start and end apart: 39 -> 60, of which waited for: 33 -> 39; matrix products, arithmetic and copies ran while one was open for 10% -> 19% of each run, Pallas kernels for 3% -> 5%
where the time goes in v2:
time: 445 us; the launch traced here: 438 us
  waiting for transfers between devices  190 us (43%)
  starting transfers between devices  67.9 us (15%)
  local copies, waits for them, and re-layouts  55.5 us (12%)
  other arithmetic  50.7 us (11%)
  matrix products  35.6 us (8%)
  Pallas kernels  21.2 us (5%)
  between operations  17.1 us (4%)
    ppermute x8, waiting for transfers between devices, group_sum(): other = lax.ppermute(own, 'x_hi', SWAP)  60.6 us
    ppermute x4, waiting for transfers between devices, ring_scatter(): far_up = lax.ppermute(far[:half], axis, up)  39.8 us
    ppermute x8, starting transfers between devices, group_sum(): other = lax.ppermute(own, 'x_hi', SWAP)  21.8 us
    pallas_call x3, Pallas kernels, weight_grads(): pl.pallas_call(body, grid=(2 * per_half,), in_specs=[pl.BlockSpec((tokens...  21.2 us
    ppermute x5, waiting for transfers between devices, sum_everywhere(): lax.ppermute(small, axis, [(i, i ^ step) for i in range(size)])  16.9 us
    ppermute x4, waiting for transfers between devices, ring_scatter(): far_down = lax.ppermute(far[half:], axis, down)  15.6 us
    ppermute x3, waiting for transfers between devices, swap_partner_rows(): return keep + lax.ppermute(send, 'x_lo', SWAP)  14.3 us
    unnamed x259, local copies, waits for them, and re-layouts  13.6 us
  transfers between devices with their start and end apart: 60, of which 39 were waited for; matrix products, arithmetic and copies ran while one was open for 19% of the time, Pallas kernels for 5%

profile of v2, /device:TPU:0, one launch (start us, length us, event | category | flops | bytes accessed | tf_op | source)
XLA Modules:
  0.0 437.6 jit_solution(7489874442258552497)
XLA Ops:
  16.0 2.3 slice_bitcast_fusion.2
  19.5 2.2 convolution_convert_fusion.5
  29.4 1.8 fusion.73
  31.4 1.9 collective-permute-done
  33.4 3.2 collective-permute-start.1
  36.6 12.3 %collective-permute-done.1 = f32[128,1024]{1,0:T(8,128)S(1)} collective-permute-done((f32[128,1024]{1,0:T(8,128)S(1)}, f32[128,1024]{1,0:T(8,128)S(1)}, u32[]{:S(2)}, u32[]{:S(2)}) %collective-permute-start.1) | collective-permute-done | bytes 524320 | tf_op jit(solution)/shard_map/ppermute | solution.py:97
  57.2 3.2 collective-permute-start.4
  60.4 12.4 %collective-permute-done.4 = f32[128,1024]{1,0:T(8,128)S(1)} collective-permute-done((f32[128,1024]{1,0:T(8,128)S(1)}, f32[128,1024]{1,0:T(8,128)S(1)}, u32[]{:S(2)}, u32[]{:S(2)}) %collective-permute-start.4) | collective-permute-done | bytes 524320 | tf_op jit(solution)/shard_map/ppermute | solution.py:97
  73.4 2.0 copy.70
  75.5 2.3 copy.71
  90.3 3.2 collective-permute-start.7
  93.5 12.5 %collective-permute-done.7 = f32[128,1024]{1,0:T(8,128)S(1)} collective-permute-done((f32[128,1024]{1,0:T(8,128)S(1)}, f32[128,1024]{1,0:T(8,128)S(1)}, u32[]{:S(2)}, u32[]{:S(2)}) %collective-permute-start.7) | collective-permute-done | bytes 524320 | tf_op jit(solution)/shard_map/ppermute | solution.py:97
  116.5 3.1 collective-permute-start.10
  119.6 6.6 %weight_grads.3 = f32[16,2,32,2304]{3,2,1,0:T(8,128)} custom-call(bf16[256,1024]{1,0:T(8,128)(2,1)} %copy-done.56, bf16[256,1024]{1,0:T(8,128)(2,1)} %copy-done.19, bf16[256,768]{1,0:T(8,128)(2,1)} %copy-done.60, bf16[256,768]{1,0:T(8,128)(2,1)} %copy-done.59, bf16[256,768]{1,0:T(8,128)(2,1)} %get-tuple-element.80.refs_4_), custom_call_target="tpu_custom_call" | custom-call | flops 1207959552 | bytes 9437184 | tf_op jit(solution)/shard_map/weight_grads/pallas_call | solution.py:140
  126.2 6.2 %collective-permute-done.10 = f32[128,1024]{1,0:T(8,128)} collective-permute-done((f32[128,1024]{1,0:T(8,128)}, f32[128,1024]{1,0:T(8,128)}, u32[]{:S(2)}, u32[]{:S(2)}) %collective-permute-start.10) | collective-permute-done | bytes 524320 | tf_op jit(solution)/shard_map/ppermute | solution.py:97
  134.1 1.9 collective-permute-done.11
  136.0 2.2 multiply_reduce_fusion
  143.2 1.8 copy.84
  145.1 1.9 bitcast_convert_fusion.1
  147.0 2.0 copy.110
  150.3 1.8 fusion.57
  160.0 3.2 collective-permute-start.13
  163.2 12.3 %collective-permute-done.13 = f32[128,1024]{1,0:T(8,128)S(1)} collective-permute-done((f32[128,1024]{1,0:T(8,128)S(1)}, f32[128,1024]{1,0:T(8,128)S(1)}, u32[]{:S(2)}, u32[]{:S(2)}) %collective-permute-start.13) | collective-permute-done | bytes 524320 | tf_op jit(solution)/shard_map/ppermute | solution.py:97
  175.7 1.9 collective-permute-done.14
  187.8 3.1 collective-permute-start.16
  190.9 1.8 copy.137.refs_7_
  196.0 1.8 copy.142.refs_4_
  197.8 9.0 %weight_grads.4 = f32[16,2,32,3840]{3,2,1,0:T(8,128)} custom-call(bf16[256,1024]{1,0:T(8,128)(2,1)} %copy-done.16, bf16[256,1024]{1,0:T(8,128)(2,1)} %copy-done.47, bf16[256,1024]{1,0:T(8,128)(2,1)} %copy-done.55, bf16[256,1024]{1,0:T(8,128)(2,1)} %copy-done.49, bf16[256,512]{1,0:T(8,128)(2,1)} %copy.142.refs_4_, bf16[256,256]{1,0:T(8,128)(2,1)} %copy.143.refs_5_, ...), custom_call_target="tpu_custom_call" | custom-call | flops 2013265920 | bytes 15728640 | tf_op jit(solution)/shard_map/weight_grads/pallas_call | solution.py:140
  206.8 2.1 add.479
  209.2 1.8 copy.134.refs_5_
  211.4 2.5 multiply_reduce_fusion.2
  213.9 2.7 fusion.150
  218.8 2.0 fusion.59
  223.4 2.0 copy.124
  233.6 5.7 %weight_grads.5 = f32[16,2,32,1536]{3,2,1,0:T(8,128)} custom-call(bf16[256,1024]{1,0:T(8,128)(2,1)} %copy-done.10, bf16[256,1024]{1,0:T(8,128)(2,1)} %copy-done.48, bf16[256,512]{1,0:T(8,128)(2,1)} %copy.145.refs_2_, bf16[256,256]{1,0:T(8,128)(2,1)} %copy.146.refs_3_, bf16[256,256]{1,0:T(8,128)(2,1)} %copy.147.refs_4_, bf16[256,512]{1,0:T(8,128)(2,1)} %copy.134.refs_5_), custom_call_target="tpu_custom_call" | custom-call | flops 805306368 | bytes 6291456 | tf_op jit(solution)/shard_map/weight_grads/pallas_call | solution.py:140
  244.0 3.6 collective-permute-start.28
  247.7 4.0 collective-permute-start.40
  252.6 12.5 %collective-permute-done.28 = f32[2,64,768]{2,1,0:T(8,128)S(1)} collective-permute-done((f32[2,64,768]{2,1,0:T(8,128)S(1)}, f32[2,64,768]{2,1,0:T(8,128)S(1)}, u32[]{:S(2)}, u32[]{:S(2)}) %collective-permute-start.28) | collective-permute-done | bytes 393248 | tf_op jit(solution)/shard_map/ppermute | solution.py:181
  265.9 3.1 collective-permute-done.40
  271.2 2.4 collective-permute-done.27
  273.6 16.6 %collective-permute-done.25 = f32[2,64,768]{2,1,0:T(8,128)S(1)} collective-permute-done((f32[2,64,768]{2,1,0:T(8,128)S(1)}, f32[2,64,768]{2,1,0:T(8,128)S(1)}, u32[]{:S(2)}, u32[]{:S(2)}) %collective-permute-start.25) | collective-permute-done | bytes 393248 | tf_op jit(solution)/shard_map/ppermute | solution.py:180
  290.2 3.2 collective-permute-start.41
  294.5 16.7 %collective-permute-done.37 = f32[2,64,768]{2,1,0:T(8,128)S(1)} collective-permute-done((f32[2,64,768]{2,1,0:T(8,128)S(1)}, f32[2,64,768]{2,1,0:T(8,128)S(1)}, u32[]{:S(2)}, u32[]{:S(2)}) %collective-permute-start.37) | collective-permute-done | bytes 393248 | tf_op jit(solution)/shard_map/ppermute | solution.py:180
  314.1 3.2 collective-permute-start.30
  317.2 10.8 %collective-permute-done.36 = f32[2,64,768]{2,1,0:T(8,128)S(1)} collective-permute-done((f32[2,64,768]{2,1,0:T(8,128)S(1)}, f32[2,64,768]{2,1,0:T(8,128)S(1)}, u32[]{:S(2)}, u32[]{:S(2)}) %collective-permute-start.36) | collective-permute-done | bytes 393248 | tf_op jit(solution)/shard_map/ppermute | solution.py:183
  328.4 5.3 %collective-permute-done.38 = f32[2,64,768]{2,1,0:T(8,128)S(1)} collective-permute-done((f32[2,64,768]{2,1,0:T(8,128)S(1)}, f32[2,64,768]{2,1,0:T(8,128)S(1)}, u32[]{:S(2)}, u32[]{:S(2)}) %collective-permute-start.38) | collective-permute-done | bytes 393248 | tf_op jit(solution)/shard_map/ppermute | solution.py:184
  333.7 1.9 collective-permute-start.34
  335.9 4.0 collective-permute-done.31
  340.0 3.3 collective-permute-start.46
  343.3 2.5 collective-permute-done.43
  345.8 3.3 collective-permute-start.35
  349.2 3.2 collective-permute-start.42
  353.5 2.2 collective-permute-start.47
  355.7 2.1 collective-permute-done.45
  357.8 2.4 collective-permute-start.19
  364.7 4.9 %collective-permute-done.19 = f32[128,1024]{1,0:T(8,128)} collective-permute-done((f32[128,1024]{1,0:T(8,128)}, f32[128,1024]{1,0:T(8,128)}, u32[]{:S(2)}, u32[]{:S(2)}) %collective-permute-start.19) | collective-permute-done | bytes 524320 | tf_op jit(solution)/shard_map/ppermute | solution.py:97
  375.0 2.1 collective-permute-done.51
  377.5 3.4 collective-permute-done.52
  382.1 4.2 collective-permute-done.53
  386.4 3.7 collective-permute-done.54
  391.8 3.5 collective-permute-done.55
  396.5 3.1 collective-permute-start.57
  409.2 6.7 %collective-permute-done.50 = f32[32,2304]{1,0:T(8,128)S(1)} collective-permute-done((f32[32,2304]{1,0:T(8,128)S(1)}, f32[32,2304]{1,0:T(8,128)S(1)}, u32[]{:S(2)}, u32[]{:S(2)}) %collective-permute-start.50) | collective-permute-done | bytes 294944 | tf_op jit(solution)/shard_map/ppermute | solution.py:163
  417.0 7.6 %collective-permute-done.49 = f32[32,3840]{1,0:T(8,128)S(1)} collective-permute-done((f32[32,3840]{1,0:T(8,128)S(1)}, f32[32,3840]{1,0:T(8,128)S(1)}, u32[]{:S(2)}, u32[]{:S(2)}) %collective-permute-start.49) | collective-permute-done | bytes 491552 | tf_op jit(solution)/shard_map/ppermute | solution.py:163
  (564 shorter events, 136.3 us)
Async XLA Ops:
  7.2 397.8 %reduce-scatter.5.cloned.1.call-start = ((), (), s32[]{:S(2)}) async-start(), calls=%async_computation.3 | async-start | bytes 10027008 | tf_op jit(solution)/shard_map/reduce_scatter | solution.py:167
  13.6 65.8 %copy-start.80 = (f32[1,1024]{1,0:T(1,128)}, f32[1,1024]{1,0:T(1,128)S(1)}, u32[]{:S(2)}) copy-start(f32[1,1024]{1,0:T(1,128)S(1)} %get-tuple-element.144) | copy-start | bytes 12292
  16.0 35.0 %copy-start.6 = (bf16[256,1024]{1,0:T(8,128)(2,1)}, bf16[256,1024]{1,0:T(8,128)(2,1)S(1)}, u32[]{:S(2)}) copy-start(bf16[256,1024]{1,0:T(8,128)(2,1)S(1)} %get-tuple-element.60) | copy-start | bytes 1572868
  29.4 24.2 %copy-start.23 = (bf16[2,128,2,256]{3,1,2,0:T(8,128)(2,1)}, bf16[2,128,2,256]{3,1,2,0:T(8,128)(2,1)S(1)}, u32[]{:S(2)}) copy-start(bf16[2,128,2,256]{3,1,2,0:T(8,128)(2,1)S(1)} %convolution_convert_fusion.3) | copy-start | bytes 786436
  31.3 2.0 collective-permute-start
  33.4 15.5 %collective-permute-start.1 = (f32[128,1024]{1,0:T(8,128)S(1)}, f32[128,1024]{1,0:T(8,128)S(1)}, u32[]{:S(2)}, u32[]{:S(2)}) collective-permute-start(f32[128,1024]{1,0:T(8,128)S(1)} %slice_add_fusion.5), channel_id=1, source_target_pairs={{0,2},{2,0},{1,3},{3,1},{4,6},{6,4},{5,7},{7,5},{8,10},{10,8},{9,1... | collective-permute-start | bytes 1572872 | tf_op jit(solution)/shard_map/ppermute | solution.py:97
  49.0 2.0 collective-permute-start.2
  55.1 2.0 collective-permute-start.3
  57.2 15.6 %collective-permute-start.4 = (f32[128,1024]{1,0:T(8,128)S(1)}, f32[128,1024]{1,0:T(8,128)S(1)}, u32[]{:S(2)}, u32[]{:S(2)}) collective-permute-start(f32[128,1024]{1,0:T(8,128)S(1)} %slice_add_fusion.4), channel_id=1, source_target_pairs={{0,2},{2,0},{1,3},{3,1},{4,6},{6,4},{5,7},{7,5},{8,10},{10,8},{9,1... | collective-permute-start | bytes 1572872 | tf_op jit(solution)/shard_map/ppermute | solution.py:97
  72.9 4.9 %collective-permute-start.5 = (f32[128,1024]{1,0:T(8,128)S(1)}, f32[128,1024]{1,0:T(8,128)}, u32[]{:S(2)}, u32[]{:S(2)}) collective-permute-start(f32[128,1024]{1,0:T(8,128)S(1)} %add.451), channel_id=1, source_target_pairs={{0,1},{1,0},{2,3},{3,2},{4,5},{5,4},{6,7},{7,6},{8,9},{9,8},{10,11... | collective-permute-start | bytes 1572872 | tf_op jit(solution)/shard_map/ppermute | solution.py:103
  88.1 2.1 collective-permute-start.6
  90.3 15.8 %collective-permute-start.7 = (f32[128,1024]{1,0:T(8,128)S(1)}, f32[128,1024]{1,0:T(8,128)S(1)}, u32[]{:S(2)}, u32[]{:S(2)}) collective-permute-start(f32[128,1024]{1,0:T(8,128)S(1)} %slice_add_fusion.3), channel_id=1, source_target_pairs={{0,2},{2,0},{1,3},{3,1},{4,6},{6,4},{5,7},{7,5},{8,10},{10,8},{9,1... | collective-permute-start | bytes 1572872 | tf_op jit(solution)/shard_map/ppermute | solution.py:97
  106.2 2.0 collective-permute-start.8
  113.6 2.0 collective-permute-start.9
  116.5 15.9 %collective-permute-start.10 = (f32[128,1024]{1,0:T(8,128)}, f32[128,1024]{1,0:T(8,128)}, u32[]{:S(2)}, u32[]{:S(2)}) collective-permute-start(f32[128,1024]{1,0:T(8,128)} %slice_add_fusion.2), channel_id=1, source_target_pairs={{0,2},{2,0},{1,3},{3,1},{4,6},{6,4},{5,7},{7,5},{8,10},{10,8},{9,1... | collective-permute-start | bytes 1572872 | tf_op jit(solution)/shard_map/ppermute | solution.py:97
  132.4 275.3 %reduce-scatter.3.cloned.1.call-start = ((), (), s32[]{:S(2)}) async-start(), calls=%async_computation.2 | async-start | bytes 16711680 | tf_op jit(solution)/shard_map/reduce_scatter | solution.py:167
  133.8 2.2 collective-permute-start.11
  157.9 20.2 %copy-start.22 = (f32[256,1024]{1,0:T(8,128)S(1)}, f32[256,1024]{1,0:T(8,128)}, u32[]{:S(2)}) copy-start(f32[256,1024]{1,0:T(8,128)} %get-tuple-element.52) | copy-start | bytes 3145732
  157.9 2.0 collective-permute-start.12
  160.0 15.5 %collective-permute-start.13 = (f32[128,1024]{1,0:T(8,128)S(1)}, f32[128,1024]{1,0:T(8,128)S(1)}, u32[]{:S(2)}, u32[]{:S(2)}) collective-permute-start(f32[128,1024]{1,0:T(8,128)S(1)} %slice_add_fusion.1), channel_id=1, source_target_pairs={{0,2},{2,0},{1,3},{3,1},{4,6},{6,4},{5,7},{7,5},{8,10},{10,8},{9,1... | collective-permute-start | bytes 1572872 | tf_op jit(solution)/shard_map/ppermute | solution.py:97
  175.6 2.0 collective-permute-start.14
  184.8 2.1 collective-permute-start.15
  187.8 19.0 %collective-permute-start.16 = (f32[128,1024]{1,0:T(8,128)}, f32[128,1024]{1,0:T(8,128)}, u32[]{:S(2)}, u32[]{:S(2)}) collective-permute-start(f32[128,1024]{1,0:T(8,128)} %slice_add_fusion), channel_id=1, source_target_pairs={{0,2},{2,0},{1,3},{3,1},{4,6},{6,4},{5,7},{7,5},{8,10},{10,8},{9,1... | collective-permute-start | bytes 1572872 | tf_op jit(solution)/shard_map/ppermute | solution.py:97
  208.9 2.4 collective-permute-start.17
  241.9 28.2 %collective-permute-start.21 = (f32[128,1024]{1,0:T(8,128)S(1)}, f32[128,1024]{1,0:T(8,128)S(1)}, u32[]{:S(2)}, u32[]{:S(2)}) collective-permute-start(f32[128,1024]{1,0:T(8,128)S(1)} %slice.567), channel_id=1, source_target_pairs={{0,1},{1,0},{2,3},{3,2},{4,5},{5,4},{6,7},{7,6},{8,9},{9,8},{10,11... | collective-permute-start | bytes 1572872 | tf_op jit(solution)/shard_map/ppermute | solution.py:96
  244.0 21.1 %collective-permute-start.28 = (f32[2,64,768]{2,1,0:T(8,128)S(1)}, f32[2,64,768]{2,1,0:T(8,128)S(1)}, u32[]{:S(2)}, u32[]{:S(2)}) collective-permute-start(f32[2,64,768]{2,1,0:T(8,128)S(1)} %get-tuple-element.68), channel_id=1, source_target_pairs={{0,12},{4,0},{8,4},{12,8},{1,13},{5,1},{9,5},{13,9},{2,14},{6,2},{... | collective-permute-start | bytes 1179656 | tf_op jit(solution)/shard_map/ppermute | solution.py:181
  247.7 21.3 %collective-permute-start.40 = (f32[2,64,768]{2,1,0:T(8,128)S(1)}, f32[2,64,768]{2,1,0:T(8,128)S(1)}, u32[]{:S(2)}, u32[]{:S(2)}) collective-permute-start(f32[2,64,768]{2,1,0:T(8,128)S(1)} %get-tuple-element.74), channel_id=1, source_target_pairs={{0,48},{16,0},{32,16},{48,32},{1,49},{17,1},{33,17},{49,33},{2,50}... | collective-permute-start | bytes 1179656 | tf_op jit(solution)/shard_map/ppermute | solution.py:181
  252.4 41.2 %collective-permute-start.18 = (f32[128,1024]{1,0:T(8,128)S(1)}, f32[128,1024]{1,0:T(8,128)S(1)}, u32[]{:S(2)}, u32[]{:S(2)}) collective-permute-start(f32[128,1024]{1,0:T(8,128)S(1)} %slice.563), channel_id=1, source_target_pairs={{0,1},{1,0},{2,3},{3,2},{4,5},{5,4},{6,7},{7,6},{8,9},{9,8},{10,11... | collective-permute-start | bytes 1572872 | tf_op jit(solution)/shard_map/ppermute | solution.py:96
  252.5 21.1 %collective-permute-start.27 = (f32[2,64,768]{2,1,0:T(8,128)S(1)}, f32[2,64,768]{2,1,0:T(8,128)S(1)}, u32[]{:S(2)}, u32[]{:S(2)}) collective-permute-start(f32[2,64,768]{2,1,0:T(8,128)S(1)} %get-tuple-element.65), channel_id=1, source_target_pairs={{0,4},{4,8},{8,12},{12,0},{1,5},{5,9},{9,13},{13,1},{2,6},{6,10},{... | collective-permute-start | bytes 1179656 | tf_op jit(solution)/shard_map/ppermute | solution.py:182
  265.1 25.1 %collective-permute-start.25 = (f32[2,64,768]{2,1,0:T(8,128)S(1)}, f32[2,64,768]{2,1,0:T(8,128)S(1)}, u32[]{:S(2)}, u32[]{:S(2)}) collective-permute-start(f32[2,64,768]{2,1,0:T(8,128)S(1)} %get-tuple-element.66), channel_id=1, source_target_pairs={{0,4},{4,8},{8,12},{12,0},{1,5},{5,9},{9,13},{13,1},{2,6},{6,10},{... | collective-permute-start | bytes 1179656 | tf_op jit(solution)/shard_map/ppermute | solution.py:180
  269.0 21.2 %collective-permute-start.29 = (f32[2,64,768]{2,1,0:T(8,128)S(1)}, f32[2,64,768]{2,1,0:T(8,128)S(1)}, u32[]{:S(2)}, u32[]{:S(2)}) collective-permute-start(f32[2,64,768]{2,1,0:T(8,128)S(1)} %fusion.111), channel_id=1, source_target_pairs={{0,12},{4,0},{8,4},{12,8},{1,13},{5,1},{9,5},{13,9},{2,14},{6,2},{... | collective-permute-start | bytes 1179656 | tf_op jit(solution)/shard_map/ppermute | solution.py:185
  270.1 42.0 %collective-permute-start.24 = (f32[2,64,768]{2,1,0:T(8,128)S(1)}, f32[2,64,768]{2,1,0:T(8,128)S(1)}, u32[]{:S(2)}, u32[]{:S(2)}) collective-permute-start(f32[2,64,768]{2,1,0:T(8,128)S(1)} %get-tuple-element.67), channel_id=1, source_target_pairs={{0,12},{4,0},{8,4},{12,8},{1,13},{5,1},{9,5},{13,9},{2,14},{6,2},{... | collective-permute-start | bytes 1179656 | tf_op jit(solution)/shard_map/ppermute | solution.py:183
  273.6 20.9 %collective-permute-start.39 = (f32[2,64,768]{2,1,0:T(8,128)S(1)}, f32[2,64,768]{2,1,0:T(8,128)S(1)}, u32[]{:S(2)}, u32[]{:S(2)}) collective-permute-start(f32[2,64,768]{2,1,0:T(8,128)S(1)} %get-tuple-element.71), channel_id=1, source_target_pairs={{0,16},{16,32},{32,48},{48,0},{1,17},{17,33},{33,49},{49,1},{2,18}... | collective-permute-start | bytes 1179656 | tf_op jit(solution)/shard_map/ppermute | solution.py:182
  290.2 21.0 %collective-permute-start.37 = (f32[2,64,768]{2,1,0:T(8,128)S(1)}, f32[2,64,768]{2,1,0:T(8,128)S(1)}, u32[]{:S(2)}, u32[]{:S(2)}) collective-permute-start(f32[2,64,768]{2,1,0:T(8,128)S(1)} %get-tuple-element.72), channel_id=1, source_target_pairs={{0,16},{16,32},{32,48},{48,0},{1,17},{17,33},{33,49},{49,1},{2,18}... | collective-permute-start | bytes 1179656 | tf_op jit(solution)/shard_map/ppermute | solution.py:180
  290.2 21.4 %collective-permute-start.41 = (f32[2,64,768]{2,1,0:T(8,128)S(1)}, f32[2,64,768]{2,1,0:T(8,128)S(1)}, u32[]{:S(2)}, u32[]{:S(2)}) collective-permute-start(f32[2,64,768]{2,1,0:T(8,128)S(1)} %fusion.105), channel_id=1, source_target_pairs={{0,48},{16,0},{32,16},{48,32},{1,49},{17,1},{33,17},{49,33},{2,50}... | collective-permute-start | bytes 1179656 | tf_op jit(solution)/shard_map/ppermute | solution.py:185
  293.6 20.0 %collective-permute-start.26 = (f32[2,64,768]{2,1,0:T(8,128)S(1)}, f32[2,64,768]{2,1,0:T(8,128)S(1)}, u32[]{:S(2)}, u32[]{:S(2)}) collective-permute-start(f32[2,64,768]{2,1,0:T(8,128)S(1)} %get-tuple-element.64), channel_id=1, source_target_pairs={{0,4},{4,8},{8,12},{12,0},{1,5},{5,9},{9,13},{13,1},{2,6},{6,10},{... | collective-permute-start | bytes 1179656 | tf_op jit(solution)/shard_map/ppermute | solution.py:184
  294.5 33.5 %collective-permute-start.36 = (f32[2,64,768]{2,1,0:T(8,128)S(1)}, f32[2,64,768]{2,1,0:T(8,128)S(1)}, u32[]{:S(2)}, u32[]{:S(2)}) collective-permute-start(f32[2,64,768]{2,1,0:T(8,128)S(1)} %get-tuple-element.73), channel_id=1, source_target_pairs={{0,48},{16,0},{32,16},{48,32},{1,49},{17,1},{33,17},{49,33},{2,50}... | collective-permute-start | bytes 1179656 | tf_op jit(solution)/shard_map/ppermute | solution.py:183
  311.2 52.2 %collective-permute-start.22 = (f32[128,1024]{1,0:T(8,128)S(1)}, f32[128,1024]{1,0:T(8,128)}, u32[]{:S(2)}, u32[]{:S(2)}) collective-permute-start(f32[128,1024]{1,0:T(8,128)S(1)} %slice_add_fusion.6), channel_id=1, source_target_pairs={{0,2},{2,0},{1,3},{3,1},{4,6},{6,4},{5,7},{7,5},{8,10},{10,8},{9,1... | collective-permute-start | bytes 1572872 | tf_op jit(solution)/shard_map/ppermute | solution.py:97
  311.7 21.9 %collective-permute-start.38 = (f32[2,64,768]{2,1,0:T(8,128)S(1)}, f32[2,64,768]{2,1,0:T(8,128)S(1)}, u32[]{:S(2)}, u32[]{:S(2)}) collective-permute-start(f32[2,64,768]{2,1,0:T(8,128)S(1)} %get-tuple-element.70), channel_id=1, source_target_pairs={{0,16},{16,32},{32,48},{48,0},{1,17},{17,33},{33,49},{49,1},{2,18}... | collective-permute-start | bytes 1179656 | tf_op jit(solution)/shard_map/ppermute | solution.py:184
  313.8 35.3 %collective-permute-start.33 = (f32[32,768]{1,0:T(8,128)S(1)}, f32[32,768]{1,0:T(8,128)S(1)}, u32[]{:S(2)}, u32[]{:S(2)}) collective-permute-start(f32[32,768]{1,0:T(8,128)S(1)} %slice_bitcast_fusion.20), channel_id=1, source_target_pairs={{0,16},{16,32},{32,48},{48,0},{1,17},{17,33},{33,49},{49,1},{2,18}... | collective-permute-start | bytes 294920 | tf_op jit(solution)/shard_map/ppermute | solution.py:182
  314.1 35.1 %collective-permute-start.30 = (f32[32,768]{1,0:T(8,128)S(1)}, f32[32,768]{1,0:T(8,128)S(1)}, u32[]{:S(2)}, u32[]{:S(2)}) collective-permute-start(f32[32,768]{1,0:T(8,128)S(1)} %slice_bitcast_fusion.24), channel_id=1, source_target_pairs={{0,48},{16,0},{32,16},{48,32},{1,49},{17,1},{33,17},{49,33},{2,50}... | collective-permute-start | bytes 294920 | tf_op jit(solution)/shard_map/ppermute | solution.py:183
  328.0 11.9 %collective-permute-start.31 = (f32[32,768]{1,0:T(8,128)S(1)}, f32[32,768]{1,0:T(8,128)S(1)}, u32[]{:S(2)}, u32[]{:S(2)}) collective-permute-start(f32[32,768]{1,0:T(8,128)S(1)} %get-tuple-element.132), channel_id=1, source_target_pairs={{0,16},{16,32},{32,48},{48,0},{1,17},{17,33},{33,49},{49,1},{2,18}... | collective-permute-start | bytes 294920 | tf_op jit(solution)/shard_map/ppermute | solution.py:180
  333.7 6.3 %collective-permute-start.34 = (f32[32,768]{1,0:T(8,128)S(1)}, f32[32,768]{1,0:T(8,128)S(1)}, u32[]{:S(2)}, u32[]{:S(2)}) collective-permute-start(f32[32,768]{1,0:T(8,128)S(1)} %get-tuple-element.133), channel_id=1, source_target_pairs={{0,48},{16,0},{32,16},{48,32},{1,49},{17,1},{33,17},{49,33},{2,50}... | collective-permute-start | bytes 294920 | tf_op jit(solution)/shard_map/ppermute | solution.py:181
  339.9 5.8 %collective-permute-start.43 = (f32[32,768]{1,0:T(8,128)S(1)}, f32[32,768]{1,0:T(8,128)S(1)}, u32[]{:S(2)}, u32[]{:S(2)}) collective-permute-start(f32[32,768]{1,0:T(8,128)S(1)} %get-tuple-element.136), channel_id=1, source_target_pairs={{0,4},{4,8},{8,12},{12,0},{1,5},{5,9},{9,13},{13,1},{2,6},{6,10},{... | collective-permute-start | bytes 294920 | tf_op jit(solution)/shard_map/ppermute | solution.py:180
  340.0 5.8 %collective-permute-start.46 = (f32[32,768]{1,0:T(8,128)S(1)}, f32[32,768]{1,0:T(8,128)S(1)}, u32[]{:S(2)}, u32[]{:S(2)}) collective-permute-start(f32[32,768]{1,0:T(8,128)S(1)} %get-tuple-element.137), channel_id=1, source_target_pairs={{0,12},{4,0},{8,4},{12,8},{1,13},{5,1},{9,5},{13,9},{2,14},{6,2},{... | collective-permute-start | bytes 294920 | tf_op jit(solution)/shard_map/ppermute | solution.py:181
  345.8 6.7 %collective-permute-start.32 = (f32[32,768]{1,0:T(8,128)S(1)}, f32[32,768]{1,0:T(8,128)S(1)}, u32[]{:S(2)}, u32[]{:S(2)}) collective-permute-start(f32[32,768]{1,0:T(8,128)S(1)} %fusion.138), channel_id=1, source_target_pairs={{0,16},{16,32},{32,48},{48,0},{1,17},{17,33},{33,49},{49,1},{2,18}... | collective-permute-start | bytes 294920 | tf_op jit(solution)/shard_map/ppermute | solution.py:184
  345.8 7.7 %collective-permute-start.35 = (f32[32,768]{1,0:T(8,128)S(1)}, f32[32,768]{1,0:T(8,128)S(1)}, u32[]{:S(2)}, u32[]{:S(2)}) collective-permute-start(f32[32,768]{1,0:T(8,128)S(1)} %fusion.135), channel_id=1, source_target_pairs={{0,48},{16,0},{32,16},{48,32},{1,49},{17,1},{33,17},{49,33},{2,50}... | collective-permute-start | bytes 294920 | tf_op jit(solution)/shard_map/ppermute | solution.py:185
  349.1 8.7 %collective-permute-start.45 = (f32[32,768]{1,0:T(8,128)S(1)}, f32[32,768]{1,0:T(8,128)S(1)}, u32[]{:S(2)}, u32[]{:S(2)}) collective-permute-start(f32[32,768]{1,0:T(8,128)S(1)} %slice_bitcast_fusion.12), channel_id=1, source_target_pairs={{0,4},{4,8},{8,12},{12,0},{1,5},{5,9},{9,13},{13,1},{2,6},{6,10},{... | collective-permute-start | bytes 294920 | tf_op jit(solution)/shard_map/ppermute | solution.py:182
  349.2 11.0 %collective-permute-start.42 = (f32[32,768]{1,0:T(8,128)S(1)}, f32[32,768]{1,0:T(8,128)S(1)}, u32[]{:S(2)}, u32[]{:S(2)}) collective-permute-start(f32[32,768]{1,0:T(8,128)S(1)} %slice_bitcast_fusion.16), channel_id=1, source_target_pairs={{0,12},{4,0},{8,4},{12,8},{1,13},{5,1},{9,5},{13,9},{2,14},{6,2},{... | collective-permute-start | bytes 294920 | tf_op jit(solution)/shard_map/ppermute | solution.py:183
  352.4 8.6 %collective-permute-start.44 = (f32[32,768]{1,0:T(8,128)S(1)}, f32[32,768]{1,0:T(8,128)S(1)}, u32[]{:S(2)}, u32[]{:S(2)}) collective-permute-start(f32[32,768]{1,0:T(8,128)S(1)} %fusion.132), channel_id=1, source_target_pairs={{0,4},{4,8},{8,12},{12,0},{1,5},{5,9},{9,13},{13,1},{2,6},{6,10},{... | collective-permute-start | bytes 294920 | tf_op jit(solution)/shard_map/ppermute | solution.py:184
  353.5 7.5 %collective-permute-start.47 = (f32[32,768]{1,0:T(8,128)S(1)}, f32[32,768]{1,0:T(8,128)S(1)}, u32[]{:S(2)}, u32[]{:S(2)}) collective-permute-start(f32[32,768]{1,0:T(8,128)S(1)} %fusion.129), channel_id=1, source_target_pairs={{0,12},{4,0},{8,4},{12,8},{1,13},{5,1},{9,5},{13,9},{2,14},{6,2},{... | collective-permute-start | bytes 294920 | tf_op jit(solution)/shard_map/ppermute | solution.py:185
  357.8 11.8 %collective-permute-start.19 = (f32[128,1024]{1,0:T(8,128)}, f32[128,1024]{1,0:T(8,128)}, u32[]{:S(2)}, u32[]{:S(2)}) collective-permute-start(f32[128,1024]{1,0:T(8,128)} %slice_add_fusion.7), channel_id=1, source_target_pairs={{0,2},{2,0},{1,3},{3,1},{4,6},{6,4},{5,7},{7,5},{8,10},{10,8},{9,1... | collective-permute-start | bytes 1572872 | tf_op jit(solution)/shard_map/ppermute | solution.py:97
  361.8 9.2 %collective-permute-start.48 = (f32[32,1536]{1,0:T(8,128)}, f32[32,1536]{1,0:T(8,128)}, u32[]{:S(2)}, u32[]{:S(2)}) collective-permute-start(f32[32,1536]{1,0:T(8,128)} %dynamic-slice_bitcast_fusion.18), channel_id=1, source_target_pairs={{0,64},{64,0},{1,65},{65,1},{2,66},{66,2},{3,67},{67,3},{4,68},{68... | collective-permute-start | bytes 589832 | tf_op jit(solution)/shard_map/ppermute | solution.py:163
  364.6 7.4 %collective-permute-start.23 = (f32[128,1024]{1,0:T(8,128)S(1)}, f32[128,1024]{1,0:T(8,128)S(1)}, u32[]{:S(2)}, u32[]{:S(2)}) collective-permute-start(f32[128,1024]{1,0:T(8,128)S(1)} %add.489), channel_id=1, source_target_pairs={{0,1},{1,0},{2,3},{3,2},{4,5},{5,4},{6,7},{7,6},{8,9},{9,8},{10,11... | collective-permute-start | bytes 1572872 | tf_op jit(solution)/shard_map/ppermute | solution.py:103
  370.9 11.0 %collective-permute-start.20 = (f32[128,1024]{1,0:T(8,128)S(1)}, f32[128,1024]{1,0:T(8,128)S(1)}, u32[]{:S(2)}, u32[]{:S(2)}) collective-permute-start(f32[128,1024]{1,0:T(8,128)S(1)} %add.486), channel_id=1, source_target_pairs={{0,1},{1,0},{2,3},{3,2},{4,5},{5,4},{6,7},{7,6},{8,9},{9,8},{10,11... | collective-permute-start | bytes 1572872 | tf_op jit(solution)/shard_map/ppermute | solution.py:103
  373.3 3.9 collective-permute-start.51
  377.2 3.8 collective-permute-start.52
  381.0 5.3 %collective-permute-start.53 = (f32[36,128]{1,0:T(8,128)S(1)}, f32[36,128]{1,0:T(8,128)S(1)}, u32[]{:S(2)}, u32[]{:S(2)}) collective-permute-start(f32[36,128]{1,0:T(8,128)S(1)} %fusion.204), channel_id=1, source_target_pairs={{0,8},{4,12},{8,0},{12,4},{1,9},{5,13},{9,1},{13,5},{2,10},{6,14},... | collective-permute-start | bytes 55304 | tf_op jit(solution)/shard_map/ppermute | solution.py:205
  386.2 3.8 collective-permute-start.54
  390.0 5.3 %collective-permute-start.55 = (f32[36,128]{1,0:T(8,128)S(1)}, f32[36,128]{1,0:T(8,128)S(1)}, u32[]{:S(2)}, u32[]{:S(2)}) collective-permute-start(f32[36,128]{1,0:T(8,128)S(1)} %add.545), channel_id=1, source_target_pairs={{0,32},{16,48},{32,0},{48,16},{1,33},{17,49},{33,1},{49,17},{2,34}... | collective-permute-start | bytes 55304 | tf_op jit(solution)/shard_map/ppermute | solution.py:205
  395.3 1.2 collective-permute-start.56
  396.5 5.3 %collective-permute-start.57 = (f32[36,128]{1,0:T(8,128)S(1)}, f32[36,128]{1,0:T(8,128)S(1)}, u32[]{:S(2)}, u32[]{:S(2)}) collective-permute-start(f32[36,128]{1,0:T(8,128)S(1)} %add.547), channel_id=1, source_target_pairs={{0,2},{2,0},{1,3},{3,1},{4,6},{6,4},{5,7},{7,5},{8,10},{10,8},{9,1... | collective-permute-start | bytes 55304 | tf_op jit(solution)/shard_map/ppermute | solution.py:208
  406.0 10.0 %collective-permute-start.50 = (f32[32,2304]{1,0:T(8,128)S(1)}, f32[32,2304]{1,0:T(8,128)S(1)}, u32[]{:S(2)}, u32[]{:S(2)}) collective-permute-start(f32[32,2304]{1,0:T(8,128)S(1)} %dynamic-slice_bitcast_fusion.17), channel_id=1, source_target_pairs={{0,64},{64,0},{1,65},{65,1},{2,66},{66,2},{3,67},{67,3},{4,68},{68... | collective-permute-start | bytes 884744 | tf_op jit(solution)/shard_map/ppermute | solution.py:163
  408.8 15.7 %collective-permute-start.49 = (f32[32,3840]{1,0:T(8,128)S(1)}, f32[32,3840]{1,0:T(8,128)S(1)}, u32[]{:S(2)}, u32[]{:S(2)}) collective-permute-start(f32[32,3840]{1,0:T(8,128)S(1)} %dynamic-slice_bitcast_fusion), channel_id=1, source_target_pairs={{0,64},{64,0},{1,65},{65,1},{2,66},{66,2},{3,67},{67,3},{4,68},{68... | collective-permute-start | bytes 1474568 | tf_op jit(solution)/shard_map/ppermute | solution.py:163
  (122 other events, 628.0 us)
Sparse Core Ops, SparseCore 0:
  132.5 90.5 reduce-scatter.4
  226.6 144.9 reduce-scatter.2
